TPU v7x, 1024 devices: a whole 4x4x32 slice. The times are simulated.
1024 devices in a mesh: section: 4 (over x), seq: 128 (over z, y_lo, core), rep: 2 (over y_hi).
Axes of the slice: x: 4, y: 4 (y_hi: 2, y_lo: 2; y = y_hi * 2 + y_lo), z: 32, core: 2. Of those that a mesh axis runs over, the one named last changes fastest.
Arguments:
- signal: bfloat16 [2, 1024, 4, 4096], P(None, 'seq', None, 'rep'), may hold values from -200 to 200, as said below
- head_proj: bfloat16 [4, 32, 128, 384], P('section', 'rep'), may hold values from -2 to 6, as said below
- record_start: int32 [2, 4], replicated, may hold values from 0 to 255
- record_pad: int32 [2, 4], replicated, may hold values from 0 to 255
Outputs:
- layer_out: bfloat16 [4, 2, 1024, 4, 4096], P('section', None, 'seq', None, 'rep')
Inputs may be any that keep to these rules, and one draw needn't show every extreme that they name: `signal`: finite. `head_proj`: finite.
All inputs are finite; a program needn't handle non-finite values.
Results may differ from a plain program's by a relative error of at most 0.015.
The roundings to bfloat16 on the way count: a program that leaves them out, or rounds other values in their place, can miss the bound.
Values may be sent and summed in bfloat16 or wider, within the bound.
A program may use at most 32 MiB of HBM per device.

v0:
```python
import math

import jax
import jax.numpy as jnp
from jax import lax
from jax.sharding import PartitionSpec as P

HEADS = 32
HEAD = 128


def extended(cells, sides, width):
    for axis, dim in sides:
        count = lax.axis_size(axis)
        ends = count - 1
        head = lax.slice_in_dim(cells, 0, width, axis=dim)
        tail = lax.slice_in_dim(cells, cells.shape[dim] - width, cells.shape[dim], axis=dim)
        cells = jnp.concatenate(
            [
                lax.ppermute(tail, axis, [(i, (i + 1) % count) for i in range(ends)]),
                cells,
                lax.ppermute(head, axis, [((i + 1) % count, i) for i in range(ends)]),
            ],
            axis=dim,
        )
    return cells


def passed_along(block, axis, distance):
    devices = range(lax.axis_size(axis))
    route = [(i - distance, i) for i in devices if i - distance in devices]
    return lax.ppermute(block, axis, route)


def masked_softmax(scores, allowed):
    scores = jnp.where(allowed, scores, -1e30)
    row_top = jnp.max(scores, axis=-1, keepdims=True)
    weights = jnp.where(allowed, jnp.exp(scores - row_top), 0.0)
    return (weights / jnp.sum(weights, axis=-1, keepdims=True)).astype(jnp.bfloat16)


def project_rows(normed, weights):
    time_rows, stations, feature_width = normed.shape
    heads_dev = weights.shape[0]
    split_rows = normed.reshape(time_rows, stations, heads_dev, feature_width // heads_dev)
    return jnp.einsum(
        "tshd,hde->tshe", split_rows, weights, preferred_element_type=jnp.float32
    ).astype(jnp.bfloat16)


def axial_layer(hidden, weights, first_step, pad_steps, time_base, total_steps):
    time_dev, stations, feature_width = hidden.shape
    head_size = weights.shape[1]
    reach = time_dev // 2
    widened = hidden.astype(jnp.float32)
    local_squares = jnp.sum(widened * widened, axis=-1, keepdims=True)
    squares = lax.psum(local_squares, "rep")
    normed = (widened * lax.rsqrt(squares / (HEADS * HEAD) + 1e-06)).astype(jnp.bfloat16)
    projected = project_rows(normed, weights)
    queries = projected[..., :head_size]
    key_value = extended(projected[..., head_size:], (("seq", 0),), reach)
    keys_all = key_value[..., :head_size]
    values_all = key_value[..., head_size:]
    scale = math.sqrt(head_size)
    scores = (
        jnp.einsum("tshd,ushd->shtu", queries, keys_all, preferred_element_type=jnp.float32) / scale
    )
    key_steps = time_base - reach + jnp.arange(time_dev + 2 * reach, dtype=jnp.int32)
    key_valid = (key_steps[None, :] >= first_step[:, None]) & (
        key_steps[None, :] < total_steps - pad_steps[:, None]
    )
    offset = jnp.arange(time_dev + 2 * reach)[None, :] - jnp.arange(time_dev)[:, None]
    in_band = (offset >= 0) & (offset <= 2 * reach)
    centre = offset == reach
    allowed = in_band[None, None] & key_valid[:, None, None, :] | centre[None, None]
    time_weights = masked_softmax(scores, allowed)
    along_time = jnp.einsum(
        "shtu,ushd->tshd", time_weights, values_all, preferred_element_type=jnp.float32
    )
    query_steps = time_base + jnp.arange(time_dev, dtype=jnp.int32)
    own_valid = (query_steps[:, None] >= first_step[None, :]) & (
        query_steps[:, None] < total_steps - pad_steps[None, :]
    )
    keys_own = projected[..., head_size : 2 * head_size]
    values_own = projected[..., 2 * head_size :]
    station_scores = (
        jnp.einsum("tshd,tzhd->thsz", queries, keys_own, preferred_element_type=jnp.float32) / scale
    )
    station_allowed = own_valid[:, None, None, :] | jnp.eye(stations, dtype=bool)[None, None]
    station_weights = masked_softmax(station_scores, station_allowed)
    across = jnp.einsum(
        "thsz,tzhd->tshd", station_weights, values_own, preferred_element_type=jnp.float32
    )
    updates = (along_time + across).reshape(time_dev, stations, feature_width)
    return (widened + updates).astype(jnp.bfloat16)


def body(signal, head_proj, record_start, record_pad):
    section_count = lax.axis_size("section")
    section_index = lax.axis_index("section")
    micro_count = signal.shape[0]
    time_dev = signal.shape[1]
    total_steps = time_dev * lax.axis_size("seq")
    time_base = lax.axis_index("seq") * time_dev
    weights = head_proj[0]
    outputs = jnp.zeros(signal.shape, jnp.bfloat16)
    arriving = jnp.zeros(signal.shape[1:], jnp.bfloat16)
    tick_count = section_count + micro_count - 1
    for tick_index in range(tick_count):
        micro_index = tick_index - section_index
        slot_index = jnp.clip(micro_index, 0, micro_count - 1)
        entering = signal[min(tick_index, micro_count - 1)]
        current = jnp.where(section_index == 0, entering, arriving)
        first_step = lax.dynamic_index_in_dim(record_start, slot_index, 0, keepdims=False)
        pad_steps = lax.dynamic_index_in_dim(record_pad, slot_index, 0, keepdims=False)
        result = axial_layer(current, weights, first_step, pad_steps, time_base, total_steps)
        chosen = (jnp.arange(micro_count) == micro_index)[:, None, None, None]
        outputs = jnp.where(chosen, result[None], outputs)
        if tick_index + 1 < tick_count:
            arriving = passed_along(result, "section", 1)
    return outputs[None]


def solution(mesh):
    return jax.shard_map(
        body,
        mesh=mesh,
        in_specs=(P(None, "seq", None, "rep"), P("section", "rep", None, None), P(), P()),
        out_specs=P("section", None, "seq", None, "rep"),
        check_vma=False,
    )
```

profile of v0, /device:TPU:770, one launch (start us, length us, event | category | flops | bytes accessed | tf_op | source)
XLA Modules:
  0.0 136.7 jit_solution(14175802839632625725)
XLA Ops:
  1.4 6.4 %psum.35 = f32[8,4,1]{0,1,2:T(4,128)S(1)} all-reduce(f32[8,4,1]{0,1,2:T(4,128)S(1)} %bitcast.218), channel_id=1, replica_groups=mesh['section'=4,'seq'=128,'rep'=2] {'rep'}, use_global_device_ids=true, to_apply=%region_1.2 | all-reduce | flops 32 | bytes 256 | tf_op jit(solution)/shard_map/psum | solution.py:57
  8.4 3.4 %collective-permute-start.1 = (bf16[4,4,16,256]{3,0,1,2:T(4,128)(2,1)S(1)}, bf16[4,4,16,256]{3,0,1,2:T(4,128)(2,1)S(1)}, u32[]{:S(2)}, u32[]{:S(2)}) collective-permute-start(bf16[4,4,16,256]{3,0,1,2:T(4,128)(2,1)S(1)} %get-tuple-element.44), channel_id=1, source_target_pairs={{2,0},{4,2},{6,4},{8,6},{10,8},{12,10},{14,12},{16,14},{18,16},{20... | collective-permute-start | bytes 393224 | tf_op jit(solution)/shard_map/ppermute | solution.py:22
  11.9 1.9 %collective-permute-start = (bf16[4,4,16,256]{3,0,1,2:T(4,128)(2,1)S(1)}, bf16[4,4,16,256]{3,0,1,2:T(4,128)(2,1)S(1)}, u32[]{:S(2)}, u32[]{:S(2)}) collective-permute-start(bf16[4,4,16,256]{3,0,1,2:T(4,128)(2,1)S(1)} %get-tuple-element.43), channel_id=1, source_target_pairs={{0,2},{2,4},{4,6},{6,8},{8,10},{10,12},{12,14},{14,16},{16,18},{18... | collective-permute-start | bytes 393224 | tf_op jit(solution)/shard_map/ppermute | solution.py:20
  16.4 3.9 %collective-permute-done = bf16[4,4,16,256]{3,0,1,2:T(4,128)(2,1)S(1)} collective-permute-done((bf16[4,4,16,256]{3,0,1,2:T(4,128)(2,1)S(1)}, bf16[4,4,16,256]{3,0,1,2:T(4,128)(2,1)S(1)}, u32[]{:S(2)}, u32[]{:S(2)}) %collective-permute-start) | collective-permute-done | bytes 131104 | tf_op jit(solution)/shard_map/ppermute | solution.py:20
  21.6 3.4 %collective-permute-start.2 = (bf16[8,4,2048]{2,0,1:T(8,128)(2,1)S(1)}, bf16[8,4,2048]{2,0,1:T(8,128)(2,1)S(1)}, u32[]{:S(2)}, u32[]{:S(2)}) collective-permute-start(bf16[8,4,2048]{2,0,1:T(8,128)(2,1)S(1)} %get-tuple-element.82), channel_id=1, source_target_pairs={{0,256},{256,512},{512,768},{1,257},{257,513},{513,769},{2,258},{2... | collective-permute-start | bytes 393224 | tf_op jit(solution)/shard_map/ppermute | solution.py:32
  25.1 3.4 %collective-permute-done.2 = bf16[8,4,2048]{2,0,1:T(8,128)(2,1)S(1)} collective-permute-done((bf16[8,4,2048]{2,0,1:T(8,128)(2,1)S(1)}, bf16[8,4,2048]{2,0,1:T(8,128)(2,1)S(1)}, u32[]{:S(2)}, u32[]{:S(2)}) %collective-permute-start.2) | collective-permute-done | bytes 131104 | tf_op jit(solution)/shard_map/ppermute | solution.py:32
  28.7 6.4 %psum.36 = f32[8,4,1]{0,1,2:T(4,128)S(1)} all-reduce(f32[8,4,1]{0,1,2:T(4,128)S(1)} %bitcast.215), channel_id=1, replica_groups=mesh['section'=4,'seq'=128,'rep'=2] {'rep'}, use_global_device_ids=true, to_apply=%region_7.8 | all-reduce | flops 32 | bytes 256 | tf_op jit(solution)/shard_map/psum | solution.py:57
  38.9 2.4 %collective-permute-start.3 = (bf16[4,4,16,256]{3,0,1,2:T(4,128)(2,1)S(1)}, bf16[4,4,16,256]{3,0,1,2:T(4,128)(2,1)S(1)}, u32[]{:S(2)}, u32[]{:S(2)}) collective-permute-start(bf16[4,4,16,256]{3,0,1,2:T(4,128)(2,1)S(1)} %get-tuple-element.38), channel_id=1, source_target_pairs={{0,2},{2,4},{4,6},{6,8},{8,10},{10,12},{12,14},{14,16},{16,18},{18... | collective-permute-start | bytes 393224 | tf_op jit(solution)/shard_map/ppermute | solution.py:20
  41.6 5.7 %collective-permute-done.3 = bf16[4,4,16,256]{3,0,1,2:T(4,128)(2,1)S(1)} collective-permute-done((bf16[4,4,16,256]{3,0,1,2:T(4,128)(2,1)S(1)}, bf16[4,4,16,256]{3,0,1,2:T(4,128)(2,1)S(1)}, u32[]{:S(2)}, u32[]{:S(2)}) %collective-permute-start.3) | collective-permute-done | bytes 131104 | tf_op jit(solution)/shard_map/ppermute | solution.py:20
  50.1 3.4 %collective-permute-start.5 = (bf16[8,4,2048]{2,0,1:T(8,128)(2,1)S(1)}, bf16[8,4,2048]{2,0,1:T(8,128)(2,1)S(1)}, u32[]{:S(2)}, u32[]{:S(2)}) collective-permute-start(bf16[8,4,2048]{2,0,1:T(8,128)(2,1)S(1)} %fusion.68), channel_id=1, source_target_pairs={{0,256},{256,512},{512,768},{1,257},{257,513},{513,769},{2,258},{2... | collective-permute-start | bytes 393224 | tf_op jit(solution)/shard_map/ppermute | solution.py:32
  54.1 2.9 %collective-permute-done.5 = bf16[8,4,2048]{2,0,1:T(8,128)(2,1)S(1)} collective-permute-done((bf16[8,4,2048]{2,0,1:T(8,128)(2,1)S(1)}, bf16[8,4,2048]{2,0,1:T(8,128)(2,1)S(1)}, u32[]{:S(2)}, u32[]{:S(2)}) %collective-permute-start.5) | collective-permute-done | bytes 131104 | tf_op jit(solution)/shard_map/ppermute | solution.py:32
  57.2 6.4 %psum.37 = f32[8,4,1]{0,1,2:T(4,128)S(1)} all-reduce(f32[8,4,1]{0,1,2:T(4,128)S(1)} %bitcast.216), channel_id=1, replica_groups=mesh['section'=4,'seq'=128,'rep'=2] {'rep'}, use_global_device_ids=true, to_apply=%region_13.14 | all-reduce | flops 32 | bytes 256 | tf_op jit(solution)/shard_map/psum | solution.py:57
  67.4 2.4 %collective-permute-start.6 = (bf16[4,4,16,256]{3,0,1,2:T(4,128)(2,1)S(1)}, bf16[4,4,16,256]{3,0,1,2:T(4,128)(2,1)S(1)}, u32[]{:S(2)}, u32[]{:S(2)}) collective-permute-start(bf16[4,4,16,256]{3,0,1,2:T(4,128)(2,1)S(1)} %get-tuple-element.33), channel_id=1, source_target_pairs={{0,2},{2,4},{4,6},{6,8},{8,10},{10,12},{12,14},{14,16},{16,18},{18... | collective-permute-start | bytes 393224 | tf_op jit(solution)/shard_map/ppermute | solution.py:20
  70.1 5.7 %collective-permute-done.6 = bf16[4,4,16,256]{3,0,1,2:T(4,128)(2,1)S(1)} collective-permute-done((bf16[4,4,16,256]{3,0,1,2:T(4,128)(2,1)S(1)}, bf16[4,4,16,256]{3,0,1,2:T(4,128)(2,1)S(1)}, u32[]{:S(2)}, u32[]{:S(2)}) %collective-permute-start.6) | collective-permute-done | bytes 131104 | tf_op jit(solution)/shard_map/ppermute | solution.py:20
  79.4 3.4 %collective-permute-start.8 = (bf16[8,4,2048]{2,0,1:T(8,128)(2,1)S(1)}, bf16[8,4,2048]{2,0,1:T(8,128)(2,1)S(1)}, u32[]{:S(2)}, u32[]{:S(2)}) collective-permute-start(bf16[8,4,2048]{2,0,1:T(8,128)(2,1)S(1)} %fusion.63), channel_id=1, source_target_pairs={{0,256},{256,512},{512,768},{1,257},{257,513},{513,769},{2,258},{2... | collective-permute-start | bytes 393224 | tf_op jit(solution)/shard_map/ppermute | solution.py:32
  84.0 2.3 %collective-permute-done.8 = bf16[8,4,2048]{2,0,1:T(8,128)(2,1)S(1)} collective-permute-done((bf16[8,4,2048]{2,0,1:T(8,128)(2,1)S(1)}, bf16[8,4,2048]{2,0,1:T(8,128)(2,1)S(1)}, u32[]{:S(2)}, u32[]{:S(2)}) %collective-permute-start.8) | collective-permute-done | bytes 131104 | tf_op jit(solution)/shard_map/ppermute | solution.py:32
  86.5 6.4 %psum.38 = f32[8,4,1]{0,1,2:T(4,128)S(1)} all-reduce(f32[8,4,1]{0,1,2:T(4,128)S(1)} %bitcast.217), channel_id=1, replica_groups=mesh['section'=4,'seq'=128,'rep'=2] {'rep'}, use_global_device_ids=true, to_apply=%region_19.20 | all-reduce | flops 32 | bytes 256 | tf_op jit(solution)/shard_map/psum | solution.py:57
  97.3 2.6 %collective-permute-start.9 = (bf16[4,4,16,256]{3,0,1,2:T(4,128)(2,1)S(1)}, bf16[4,4,16,256]{3,0,1,2:T(4,128)(2,1)S(1)}, u32[]{:S(2)}, u32[]{:S(2)}) collective-permute-start(bf16[4,4,16,256]{3,0,1,2:T(4,128)(2,1)S(1)} %get-tuple-element.28), channel_id=1, source_target_pairs={{0,2},{2,4},{4,6},{6,8},{8,10},{10,12},{12,14},{14,16},{16,18},{18... | collective-permute-start | bytes 393224 | tf_op jit(solution)/shard_map/ppermute | solution.py:20
  100.2 5.5 %collective-permute-done.9 = bf16[4,4,16,256]{3,0,1,2:T(4,128)(2,1)S(1)} collective-permute-done((bf16[4,4,16,256]{3,0,1,2:T(4,128)(2,1)S(1)}, bf16[4,4,16,256]{3,0,1,2:T(4,128)(2,1)S(1)}, u32[]{:S(2)}, u32[]{:S(2)}) %collective-permute-start.9) | collective-permute-done | bytes 131104 | tf_op jit(solution)/shard_map/ppermute | solution.py:20
  108.5 3.4 %collective-permute-start.11 = (bf16[8,4,2048]{2,0,1:T(8,128)(2,1)S(1)}, bf16[8,4,2048]{2,0,1:T(8,128)(2,1)S(1)}, u32[]{:S(2)}, u32[]{:S(2)}) collective-permute-start(bf16[8,4,2048]{2,0,1:T(8,128)(2,1)S(1)} %fusion.58), channel_id=1, source_target_pairs={{0,256},{256,512},{512,768},{1,257},{257,513},{513,769},{2,258},{2... | collective-permute-start | bytes 393224 | tf_op jit(solution)/shard_map/ppermute | solution.py:32
  112.5 2.9 %collective-permute-done.11 = bf16[8,4,2048]{2,0,1:T(8,128)(2,1)S(1)} collective-permute-done((bf16[8,4,2048]{2,0,1:T(8,128)(2,1)S(1)}, bf16[8,4,2048]{2,0,1:T(8,128)(2,1)S(1)}, u32[]{:S(2)}, u32[]{:S(2)}) %collective-permute-start.11) | collective-permute-done | bytes 131104 | tf_op jit(solution)/shard_map/ppermute | solution.py:32
  115.6 6.4 %psum.39 = f32[8,4,1]{0,1,2:T(4,128)S(1)} all-reduce(f32[8,4,1]{0,1,2:T(4,128)S(1)} %bitcast.214), channel_id=1, replica_groups=mesh['section'=4,'seq'=128,'rep'=2] {'rep'}, use_global_device_ids=true, to_apply=%region_25.26 | all-reduce | flops 32 | bytes 256 | tf_op jit(solution)/shard_map/psum | solution.py:57
  125.8 2.4 %collective-permute-start.12 = (bf16[4,4,16,256]{3,0,1,2:T(4,128)(2,1)S(1)}, bf16[4,4,16,256]{3,0,1,2:T(4,128)(2,1)S(1)}, u32[]{:S(2)}, u32[]{:S(2)}) collective-permute-start(bf16[4,4,16,256]{3,0,1,2:T(4,128)(2,1)S(1)} %get-tuple-element.23), channel_id=1, source_target_pairs={{0,2},{2,4},{4,6},{6,8},{8,10},{10,12},{12,14},{14,16},{16,18},{18... | collective-permute-start | bytes 393224 | tf_op jit(solution)/shard_map/ppermute | solution.py:20
  128.5 5.7 %collective-permute-done.12 = bf16[4,4,16,256]{3,0,1,2:T(4,128)(2,1)S(1)} collective-permute-done((bf16[4,4,16,256]{3,0,1,2:T(4,128)(2,1)S(1)}, bf16[4,4,16,256]{3,0,1,2:T(4,128)(2,1)S(1)}, u32[]{:S(2)}, u32[]{:S(2)}) %collective-permute-start.12) | collective-permute-done | bytes 131104 | tf_op jit(solution)/shard_map/ppermute | solution.py:20
  (130 shorter events, 36.9 us)
Async XLA Ops:
  0.0 7.9 %copy-start = (bf16[1,16,128,384]{3,2,1,0:T(8,128)(2,1)S(1)}, bf16[1,16,128,384]{3,2,1,0:T(8,128)(2,1)}, u32[]{:S(2)}) copy-start(bf16[1,16,128,384]{3,2,1,0:T(8,128)(2,1)} %param.5) | copy-start | bytes 4718596
  8.3 6.3 %copy-start.1 = (s32[2,4]{1,0:T(2,128)S(1)}, s32[2,4]{1,0:T(2,128)}, u32[]{:S(2)}) copy-start(s32[2,4]{1,0:T(2,128)} %param.6) | copy-start | bytes 100
  8.3 6.3 %copy-start.2 = (s32[2,4]{1,0:T(2,128)S(1)}, s32[2,4]{1,0:T(2,128)}, u32[]{:S(2)}) copy-start(s32[2,4]{1,0:T(2,128)} %param.7) | copy-start | bytes 100
  8.4 7.9 %collective-permute-start.1 = (bf16[4,4,16,256]{3,0,1,2:T(4,128)(2,1)S(1)}, bf16[4,4,16,256]{3,0,1,2:T(4,128)(2,1)S(1)}, u32[]{:S(2)}, u32[]{:S(2)}) collective-permute-start(bf16[4,4,16,256]{3,0,1,2:T(4,128)(2,1)S(1)} %get-tuple-element.44), channel_id=1, source_target_pairs={{2,0},{4,2},{6,4},{8,6},{10,8},{12,10},{14,12},{16,14},{18,16},{20... | collective-permute-start | bytes 393224 | tf_op jit(solution)/shard_map/ppermute | solution.py:22
  11.9 8.4 %collective-permute-start = (bf16[4,4,16,256]{3,0,1,2:T(4,128)(2,1)S(1)}, bf16[4,4,16,256]{3,0,1,2:T(4,128)(2,1)S(1)}, u32[]{:S(2)}, u32[]{:S(2)}) collective-permute-start(bf16[4,4,16,256]{3,0,1,2:T(4,128)(2,1)S(1)} %get-tuple-element.43), channel_id=1, source_target_pairs={{0,2},{2,4},{4,6},{6,8},{8,10},{10,12},{12,14},{14,16},{16,18},{18... | collective-permute-start | bytes 393224 | tf_op jit(solution)/shard_map/ppermute | solution.py:20
  21.6 6.9 %collective-permute-start.2 = (bf16[8,4,2048]{2,0,1:T(8,128)(2,1)S(1)}, bf16[8,4,2048]{2,0,1:T(8,128)(2,1)S(1)}, u32[]{:S(2)}, u32[]{:S(2)}) collective-permute-start(bf16[8,4,2048]{2,0,1:T(8,128)(2,1)S(1)} %get-tuple-element.82), channel_id=1, source_target_pairs={{0,256},{256,512},{512,768},{1,257},{257,513},{513,769},{2,258},{2... | collective-permute-start | bytes 393224 | tf_op jit(solution)/shard_map/ppermute | solution.py:32
  37.0 4.6 %collective-permute-start.4 = (bf16[4,4,16,256]{3,0,1,2:T(4,128)(2,1)S(1)}, bf16[4,4,16,256]{3,0,1,2:T(4,128)(2,1)S(1)}, u32[]{:S(2)}, u32[]{:S(2)}) collective-permute-start(bf16[4,4,16,256]{3,0,1,2:T(4,128)(2,1)S(1)} %get-tuple-element.39), channel_id=1, source_target_pairs={{2,0},{4,2},{6,4},{8,6},{10,8},{12,10},{14,12},{16,14},{18,16},{20... | collective-permute-start | bytes 393224 | tf_op jit(solution)/shard_map/ppermute | solution.py:22
  38.9 8.4 %collective-permute-start.3 = (bf16[4,4,16,256]{3,0,1,2:T(4,128)(2,1)S(1)}, bf16[4,4,16,256]{3,0,1,2:T(4,128)(2,1)S(1)}, u32[]{:S(2)}, u32[]{:S(2)}) collective-permute-start(bf16[4,4,16,256]{3,0,1,2:T(4,128)(2,1)S(1)} %get-tuple-element.38), channel_id=1, source_target_pairs={{0,2},{2,4},{4,6},{6,8},{8,10},{10,12},{12,14},{14,16},{16,18},{18... | collective-permute-start | bytes 393224 | tf_op jit(solution)/shard_map/ppermute | solution.py:20
  50.1 6.9 %collective-permute-start.5 = (bf16[8,4,2048]{2,0,1:T(8,128)(2,1)S(1)}, bf16[8,4,2048]{2,0,1:T(8,128)(2,1)S(1)}, u32[]{:S(2)}, u32[]{:S(2)}) collective-permute-start(bf16[8,4,2048]{2,0,1:T(8,128)(2,1)S(1)} %fusion.68), channel_id=1, source_target_pairs={{0,256},{256,512},{512,768},{1,257},{257,513},{513,769},{2,258},{2... | collective-permute-start | bytes 393224 | tf_op jit(solution)/shard_map/ppermute | solution.py:32
  65.5 4.6 %collective-permute-start.7 = (bf16[4,4,16,256]{3,0,1,2:T(4,128)(2,1)S(1)}, bf16[4,4,16,256]{3,0,1,2:T(4,128)(2,1)S(1)}, u32[]{:S(2)}, u32[]{:S(2)}) collective-permute-start(bf16[4,4,16,256]{3,0,1,2:T(4,128)(2,1)S(1)} %get-tuple-element.34), channel_id=1, source_target_pairs={{2,0},{4,2},{6,4},{8,6},{10,8},{12,10},{14,12},{16,14},{18,16},{20... | collective-permute-start | bytes 393224 | tf_op jit(solution)/shard_map/ppermute | solution.py:22
  67.4 8.4 %collective-permute-start.6 = (bf16[4,4,16,256]{3,0,1,2:T(4,128)(2,1)S(1)}, bf16[4,4,16,256]{3,0,1,2:T(4,128)(2,1)S(1)}, u32[]{:S(2)}, u32[]{:S(2)}) collective-permute-start(bf16[4,4,16,256]{3,0,1,2:T(4,128)(2,1)S(1)} %get-tuple-element.33), channel_id=1, source_target_pairs={{0,2},{2,4},{4,6},{6,8},{8,10},{10,12},{12,14},{14,16},{16,18},{18... | collective-permute-start | bytes 393224 | tf_op jit(solution)/shard_map/ppermute | solution.py:20
  79.4 6.9 %collective-permute-start.8 = (bf16[8,4,2048]{2,0,1:T(8,128)(2,1)S(1)}, bf16[8,4,2048]{2,0,1:T(8,128)(2,1)S(1)}, u32[]{:S(2)}, u32[]{:S(2)}) collective-permute-start(bf16[8,4,2048]{2,0,1:T(8,128)(2,1)S(1)} %fusion.63), channel_id=1, source_target_pairs={{0,256},{256,512},{512,768},{1,257},{257,513},{513,769},{2,258},{2... | collective-permute-start | bytes 393224 | tf_op jit(solution)/shard_map/ppermute | solution.py:32
  95.4 4.8 %collective-permute-start.10 = (bf16[4,4,16,256]{3,0,1,2:T(4,128)(2,1)}, bf16[4,4,16,256]{3,0,1,2:T(4,128)(2,1)S(1)}, u32[]{:S(2)}, u32[]{:S(2)}) collective-permute-start(bf16[4,4,16,256]{3,0,1,2:T(4,128)(2,1)} %get-tuple-element.29), channel_id=1, source_target_pairs={{2,0},{4,2},{6,4},{8,6},{10,8},{12,10},{14,12},{16,14},{18,16},{20... | collective-permute-start | bytes 393224 | tf_op jit(solution)/shard_map/ppermute | solution.py:22
  97.3 8.4 %collective-permute-start.9 = (bf16[4,4,16,256]{3,0,1,2:T(4,128)(2,1)S(1)}, bf16[4,4,16,256]{3,0,1,2:T(4,128)(2,1)S(1)}, u32[]{:S(2)}, u32[]{:S(2)}) collective-permute-start(bf16[4,4,16,256]{3,0,1,2:T(4,128)(2,1)S(1)} %get-tuple-element.28), channel_id=1, source_target_pairs={{0,2},{2,4},{4,6},{6,8},{8,10},{10,12},{12,14},{14,16},{16,18},{18... | collective-permute-start | bytes 393224 | tf_op jit(solution)/shard_map/ppermute | solution.py:20
  108.5 6.9 %collective-permute-start.11 = (bf16[8,4,2048]{2,0,1:T(8,128)(2,1)S(1)}, bf16[8,4,2048]{2,0,1:T(8,128)(2,1)S(1)}, u32[]{:S(2)}, u32[]{:S(2)}) collective-permute-start(bf16[8,4,2048]{2,0,1:T(8,128)(2,1)S(1)} %fusion.58), channel_id=1, source_target_pairs={{0,256},{256,512},{512,768},{1,257},{257,513},{513,769},{2,258},{2... | collective-permute-start | bytes 393224 | tf_op jit(solution)/shard_map/ppermute | solution.py:32
  123.9 4.6 %collective-permute-start.13 = (bf16[4,4,16,256]{3,0,1,2:T(4,128)(2,1)S(1)}, bf16[4,4,16,256]{3,0,1,2:T(4,128)(2,1)S(1)}, u32[]{:S(2)}, u32[]{:S(2)}) collective-permute-start(bf16[4,4,16,256]{3,0,1,2:T(4,128)(2,1)S(1)} %get-tuple-element.24), channel_id=1, source_target_pairs={{2,0},{4,2},{6,4},{8,6},{10,8},{12,10},{14,12},{16,14},{18,16},{20... | collective-permute-start | bytes 393224 | tf_op jit(solution)/shard_map/ppermute | solution.py:22
  125.8 8.4 %collective-permute-start.12 = (bf16[4,4,16,256]{3,0,1,2:T(4,128)(2,1)S(1)}, bf16[4,4,16,256]{3,0,1,2:T(4,128)(2,1)S(1)}, u32[]{:S(2)}, u32[]{:S(2)}) collective-permute-start(bf16[4,4,16,256]{3,0,1,2:T(4,128)(2,1)S(1)} %get-tuple-element.23), channel_id=1, source_target_pairs={{0,2},{2,4},{4,6},{6,8},{8,10},{10,12},{12,14},{14,16},{16,18},{18... | collective-permute-start | bytes 393224 | tf_op jit(solution)/shard_map/ppermute | solution.py:20
  134.7 0.9 copy-start.3
  134.7 0.9 copy-start.4
  134.7 0.9 copy-start.5
  134.7 0.9 copy-start.6
  134.8 0.9 copy-start.7
where the time goes:
time: 137 us
  waiting for transfers between devices  38 us (28%)
  starting transfers between devices  36.4 us (27%)
  blocking collectives  32.1 us (23%)
  matrix products  14.2 us (10%)
  other arithmetic  8.13 us (6%)
  local copies, waits for them, and re-layouts  6.93 us (5%)
    psum x5, blocking collectives, axial_layer(): squares = lax.psum(local_squares, 'rep')  32.1 us
    ppermute x5, waiting for transfers between devices, extended(): lax.ppermute(tail, axis, [(i, (i + 1) % count) for i in range(ends)])  26.5 us
    ppermute x4, starting transfers between devices, passed_along(): return lax.ppermute(block, axis, route)  13.6 us
    ppermute x5, starting transfers between devices, extended(): lax.ppermute(tail, axis, [(i, (i + 1) % count) for i in range(ends)])  11.7 us
    ppermute x4, waiting for transfers between devices, passed_along(): return lax.ppermute(block, axis, route)  11.5 us
    ppermute x5, starting transfers between devices, extended(): lax.ppermute(head, axis, [((i + 1) % count, i) for i in range(ends)])  11.1 us
    sub x5, matrix products, masked_softmax(): weights = jnp.where(allowed, jnp.exp(scores - row_top), 0.0)  4.72 us
    dot_general x5, matrix products, axial_layer(): jnp.einsum('shtu,ushd->tshd', time_weights, values_all, preferred_element...  4.56 us
  transfers between devices with their start and end apart: 14, of which 9 were waited for; matrix products, arithmetic and copies ran while one was open for 4% of the time, Pallas kernels for 0%

commit v1 on v0

v1 whole, which is shorter than its diff:
```python
import math

import jax
import jax.numpy as jnp
from jax import lax
from jax.experimental import pallas as pl
from jax.experimental.pallas import tpu as pltpu
from jax.sharding import PartitionSpec as P

HEADS = 32
HEAD = 128
REACH = 4
MESH = pl.DeviceIdType.MESH
F32 = jnp.float32
BF16 = jnp.bfloat16
GROUP = 4
MASKED = -1e30


def kernel(
    sig_hbm, w_hbm, start_hbm, pad_hbm, out,
    sig, hid, w, start, pad, qkv, halo_kv, pin, pout, bias_t, bias_s,
    in_sem, own_s, own_r, halo_s, halo_r, p_s, p_r,
):
    micro, own, width = out.shape
    heads = width // HEAD
    chunks = heads // GROUP
    half = own // 2
    sections = lax.axis_size("section")
    count = lax.axis_size("seq")
    s = lax.axis_index("section")
    j = lax.axis_index("seq")
    r = lax.axis_index("rep")
    left = jnp.maximum(j - 1, 0)
    right = jnp.minimum(j + 1, count - 1)
    has_left = j > 0
    has_right = j < count - 1
    other = 1 - r
    following = lax.rem(s + 1, sections)
    before = jnp.maximum(s - 1, 0)
    first = s == 0
    last = s == sections - 1

    w_copy = pltpu.make_async_copy(w_hbm, w, in_sem.at[0])
    sig_copy = pltpu.make_async_copy(sig_hbm, sig, in_sem.at[1])
    start_copy = pltpu.make_async_copy(start_hbm, start, in_sem.at[2])
    pad_copy = pltpu.make_async_copy(pad_hbm, pad, in_sem.at[3])
    sig_copy.start()
    w_copy.start()
    start_copy.start()
    pad_copy.start()

    barrier = pltpu.get_barrier_semaphore()

    def greet(device):
        pl.semaphore_signal(barrier, inc=1, device_id=device, device_id_type=MESH)

    greet((before, j, other))

    @pl.when(has_left)
    def _():
        greet((s, left, r))
        greet((before, left, other))

    @pl.when(has_right)
    def _():
        greet((s, right, r))
        greet((before, right, other))

    @pl.when(jnp.logical_not(first))
    def _():
        greet((before, j, r))

    def lanes(c):
        return pl.ds(c * GROUP * HEAD, GROUP * HEAD)

    def own_copy(m, c):
        return pltpu.make_async_remote_copy(
            src_ref=out.at[m, :, lanes(c)],
            dst_ref=hid.at[m, pl.ds(0, own), lanes(c)],
            send_sem=own_s.at[m, c],
            recv_sem=own_r.at[m, c],
            device_id=(following, j, r),
            device_id_type=MESH,
        )

    def halo_copy(m, c, side):
        return pltpu.make_async_remote_copy(
            src_ref=hid.at[m, pl.ds(side * half, half), lanes(c)],
            dst_ref=hid.at[m, pl.ds(own + (1 - side) * half, half), lanes(c)],
            send_sem=halo_s.at[m, c, side],
            recv_sem=halo_r.at[m, c, side],
            device_id=(s, right if side else left, r),
            device_id_type=MESH,
        )

    def p_copy(k, m, section, i):
        src, dst, place = (
            (pl.ds(0, half), pl.ds(own + half, half), left),
            (pl.ds(half, half), pl.ds(own, half), right),
            (pl.ds(0, own), pl.ds(0, own), j),
        )[i]
        return pltpu.make_async_remote_copy(
            src_ref=pout.at[k, m, src],
            dst_ref=pin.at[m, dst],
            send_sem=p_s.at[k, m, i],
            recv_sem=p_r.at[m, i],
            device_id=(section, place, other),
            device_id_type=MESH,
        )

    def sides(to_left, to_right):
        @pl.when(has_left)
        def _():
            to_left()

        @pl.when(has_right)
        def _():
            to_right()

    def forward_halo(m, c):
        sides(lambda: halo_copy(m, c, 0).start(), lambda: halo_copy(m, c, 1).start())

    def send_p(k, m, section):
        p_copy(k, m, section, 2).start()
        sides(
            lambda: p_copy(k, m, section, 0).start(),
            lambda: p_copy(k, m, section, 1).start(),
        )

    def wait_sent_p(k, m, section):
        p_copy(k, m, section, 2).wait_send()
        sides(
            lambda: p_copy(k, m, section, 0).wait_send(),
            lambda: p_copy(k, m, section, 1).wait_send(),
        )

    def squares(m, rows, heads_of):
        total = None
        for h in heads_of:
            x = hid[m, rows, h * HEAD : (h + 1) * HEAD].astype(F32)
            total = x * x if total is None else total + x * x
        return total

    every = range(heads)

    @pl.when(jnp.logical_not(has_left))
    def _():
        hid[:, pl.ds(own, half), :] = jnp.zeros((micro, half, width), BF16)
        pin[:, pl.ds(own, half), :] = jnp.zeros((micro, half, HEAD), F32)

    @pl.when(jnp.logical_not(has_right))
    def _():
        hid[:, pl.ds(own + half, half), :] = jnp.zeros((micro, half, width), BF16)
        pin[:, pl.ds(own + half, half), :] = jnp.zeros((micro, half, HEAD), F32)

    sig_copy.wait()

    @pl.when(first)
    def _():
        for m in range(micro):
            partial = jnp.zeros((own, HEAD), F32)
            for h in every:
                x = sig[m, :, :, h * HEAD : (h + 1) * HEAD].astype(F32).reshape(own, HEAD)
                partial = partial + x * x
                hid[m, pl.ds(0, own), h * HEAD : (h + 1) * HEAD] = x.astype(BF16)
            pout[0, m] = partial

    beside = has_left.astype(jnp.int32) + has_right.astype(jnp.int32)
    receivers = beside + jnp.where(last, 0, 2 + beside) + jnp.where(first, 1 + beside, 0)
    pl.semaphore_wait(barrier, receivers)

    @pl.when(first)
    def _():
        for m in range(micro):
            send_p(0, m, s)
        for m in range(micro):
            for c in range(chunks):
                forward_halo(m, c)

    start_copy.wait()
    pad_copy.wait()
    row = lax.broadcasted_iota(jnp.int32, (2 * own, 4 * own), 0)
    col = lax.broadcasted_iota(jnp.int32, (2 * own, 4 * own), 1) & (own - 1)
    key_time = (row >> 2) - jnp.where(row < own, 0, jnp.where(row < own + half, 12, 4))
    key_station = row & 3
    query_time = col >> 2
    query_station = col & 3
    step = j * (own // 4) + key_time
    total_steps = count * (own // 4)
    for m in range(micro):
        begin = jnp.zeros_like(row)
        end = jnp.zeros_like(row)
        for z in range(4):
            begin = jnp.where(key_station == z, start[m, z], begin)
            end = jnp.where(key_station == z, total_steps - pad[m, z], end)
        valid = (step >= begin) & (step < end)
        same_time = key_time == query_time
        same_station = key_station == query_station
        near = jnp.abs(key_time - query_time) <= REACH
        bias_t[m] = jnp.where(same_station & near & (valid | same_time), 0.0, MASKED)
        keep = same_time & (valid | same_station)
        bias_s[m] = jnp.where(keep, 0.0, MASKED)[:own]

    w_copy.wait()
    scale = math.log2(math.e) / math.sqrt(HEAD)

    def inverse(m, rows):
        total = jnp.sum(squares(m, rows, every) + pin[m, rows], axis=-1, keepdims=True)
        return jnp.broadcast_to(lax.rsqrt(total / (HEADS * HEAD) + 1e-06), (own, HEAD))

    def normed(m, rows, h, inv):
        x = hid[m, rows, h * HEAD : (h + 1) * HEAD]
        return (x.astype(F32) * inv).astype(BF16)

    @pl.loop(0, micro)
    def _(m):
        @pl.when(jnp.logical_not(first))
        def _():
            for c in range(chunks):
                own_copy(m, c).wait_recv()
                forward_halo(m, c)

        p_copy(1, m, following, 2).wait_recv()
        inv = inverse(m, pl.ds(0, own))
        for h in every:
            x = normed(m, pl.ds(0, own), h, inv)
            qkv[h] = jnp.dot(x, w[h], preferred_element_type=F32).astype(BF16)

        def arrived(side):
            p_copy(1, m, following, side).wait_recv()
            for c in range(chunks):
                halo_copy(m, c, side).wait_recv()

        sides(lambda: arrived(1), lambda: arrived(0))
        inv = inverse(m, pl.ds(own, own))
        for h in every:
            x = normed(m, pl.ds(own, own), h, inv)
            halo_kv[h] = jnp.dot(x, w[h, :, HEAD:], preferred_element_type=F32).astype(BF16)
        sent = jnp.zeros((own, HEAD), F32)
        for c in range(chunks):
            queries, keys, values = [], [], []
            blank = jnp.zeros((own, HEAD), BF16)
            for i in range(GROUP):
                h = c * GROUP + i
                q = qkv[h, :, :HEAD]
                queries.append(
                    jnp.concatenate([q if i == n else blank for n in range(GROUP)], axis=1)
                )
                k = qkv[h, :, HEAD : 2 * HEAD]
                keys.append(jnp.concatenate([k, halo_kv[h, :, :HEAD]], axis=0))
                v = qkv[h, :, 2 * HEAD :]
                values.append(jnp.concatenate([v, halo_kv[h, :, HEAD:], v], axis=0))
            scores = lax.dot_general(
                jnp.concatenate(keys, axis=1),
                jnp.concatenate(queries, axis=0),
                (((1,), (1,)), ((), ())),
                preferred_element_type=F32,
            ) * scale
            along = scores + bias_t[m]
            along = jnp.exp2(along - jnp.max(along, axis=0, keepdims=True))
            along = along * (1.0 / jnp.sum(along, axis=0, keepdims=True))
            across = scores[:own] + bias_s[m]
            across = jnp.exp2(across - jnp.max(across, axis=0, keepdims=True))
            across = across * (1.0 / jnp.sum(across, axis=0, keepdims=True))
            mix = jnp.transpose(jnp.concatenate([along, across], axis=0)).astype(BF16)
            for i in range(GROUP):
                h = c * GROUP + i
                update = jnp.dot(
                    mix[i * own : (i + 1) * own], values[i], preferred_element_type=F32
                )
                x = hid[m, pl.ds(0, own), h * HEAD : (h + 1) * HEAD].astype(F32)
                y = (x + update).astype(BF16)
                out[m, :, h * HEAD : (h + 1) * HEAD] = y
                y = y.astype(F32)
                sent = sent + y * y

            @pl.when(jnp.logical_not(last))
            def _():
                own_copy(m, c).start()

        @pl.when(jnp.logical_not(last))
        def _():
            pout[1, m] = sent
            send_p(1, m, following)

    def sent_halo(side):
        for m in range(micro):
            for c in range(chunks):
                halo_copy(m, c, side).wait_send()

    sides(lambda: sent_halo(0), lambda: sent_halo(1))

    @pl.when(first)
    def _():
        for m in range(micro):
            wait_sent_p(0, m, s)

    @pl.when(jnp.logical_not(last))
    def _():
        for m in range(micro):
            for c in range(chunks):
                own_copy(m, c).wait_send()
            wait_sent_p(1, m, following)


def body(signal, head_proj, record_start, record_pad):
    micro, times, stations, width = signal.shape
    own = times * stations
    heads = width // HEAD
    chunks = heads // GROUP
    dma = pltpu.SemaphoreType.DMA
    vmem = pl.BlockSpec(memory_space=pltpu.VMEM)
    hbm = pl.BlockSpec(memory_space=pltpu.HBM)
    result = pl.pallas_call(
        kernel,
        name="relay",
        out_shape=jax.ShapeDtypeStruct((micro, own, width), BF16),
        in_specs=[hbm] * 4,
        out_specs=vmem,
        scratch_shapes=[
            pltpu.VMEM(signal.shape, BF16),
            pltpu.VMEM((micro, 2 * own, width), BF16),
            pltpu.VMEM((heads, HEAD, 3 * HEAD), BF16),
            pltpu.SMEM(record_start.shape, jnp.int32),
            pltpu.SMEM(record_pad.shape, jnp.int32),
            pltpu.VMEM((heads, own, 3 * HEAD), BF16),
            pltpu.VMEM((heads, own, 2 * HEAD), BF16),
            pltpu.VMEM((micro, 2 * own, HEAD), F32),
            pltpu.VMEM((2, micro, own, HEAD), F32),
            pltpu.VMEM((micro, 2 * own, 4 * own), F32),
            pltpu.VMEM((micro, own, 4 * own), F32),
            dma((4,)),
            dma((micro, chunks)),
            dma((micro, chunks)),
            dma((micro, chunks, 2)),
            dma((micro, chunks, 2)),
            dma((2, micro, 3)),
            dma((micro, 3)),
        ],
        compiler_params=pltpu.CompilerParams(
            collective_id=0, has_side_effects=True, vmem_limit_bytes=40 * 2**20
        ),
    )(*[pltpu.with_memory_space_constraint(x, pltpu.HBM) for x in (signal, head_proj[0], record_start, record_pad)])
    return result.reshape(1, micro, times, stations, width)


def solution(mesh):
    return jax.shard_map(
        body,
        mesh=mesh,
        in_specs=(P(None, "seq", None, "rep"), P("section", "rep", None, None), P(), P()),
        out_specs=P("section", None, "seq", None, "rep"),
        check_vma=False,
    )
```

time: 137 us -> 49.2 us (0.36)
  the two profiles are of different devices: /device:TPU:770 before, /device:TPU:7 now
where the time goes in v1:
time: 49.2 us; the launch traced here: 49.1 us
  Pallas kernels  48.2 us (98%)
  local copies, waits for them, and re-layouts  0.8 us (2%)
    pallas_call x1, Pallas kernels, body(): pl.pallas_call(kernel, name='relay', out_shape=jax.ShapeDtypeStruct((micr...  48.2 us

profile of v1, /device:TPU:7, one launch (start us, length us, event | category | flops | bytes accessed | tf_op | source)
XLA Modules:
  0.0 49.1 jit_solution(10336563547255051516)
XLA Ops:
  0.0 48.2 %relay.1 = bf16[2,32,2048]{2,1,0:T(8,128)(2,1)S(1)} custom-call(bf16[2,8,4,2048]{3,2,1,0:T(4,128)(2,1)} %sig_hbm.1, bf16[16,128,384]{2,1,0:T(8,128)(2,1)} %bitcast.1, s32[2,4]{1,0:T(2,128)} %start_hbm.1, s32[2,4]{1,0:T(2,128)} %pad_hbm.1), custom_call_target="tpu_custom_call" | custom-call | tf_op jit(solution)/shard_map/relay/pallas_call | solution.py:315
  48.3 0.8 %reshape.3 = bf16[1,2,8,4,2048]{4,3,2,1,0:T(4,128)(2,1)} reshape(bf16[2,32,2048]{2,1,0:T(8,128)(2,1)S(1)} %relay.1) | data formatting | bytes 524288 | tf_op jit(solution)/shard_map/reshape | solution.py:345

commit v2 on v1

--- a/solution.py
+++ b/solution.py
@@ -71,6 +71,14 @@
     def _():
         greet((before, j, r))
 
+        @pl.when(has_left)
+        def _():
+            greet((before, left, r))
+
+        @pl.when(has_right)
+        def _():
+            greet((before, right, r))
+
     def lanes(c):
         return pl.ds(c * GROUP * HEAD, GROUP * HEAD)
 
@@ -94,7 +102,7 @@
             device_id_type=MESH,
         )
 
-    def p_copy(k, m, section, i):
+    def p_copy(k, m, section, i, rep):
         src, dst, place = (
             (pl.ds(0, half), pl.ds(own + half, half), left),
             (pl.ds(half, half), pl.ds(own, half), right),
@@ -102,10 +110,10 @@
         )[i]
         return pltpu.make_async_remote_copy(
             src_ref=pout.at[k, m, src],
-            dst_ref=pin.at[m, dst],
-            send_sem=p_s.at[k, m, i],
-            recv_sem=p_r.at[m, i],
-            device_id=(section, place, other),
+            dst_ref=pin.at[rep, m, dst],
+            send_sem=p_s.at[k, m, i, rep],
+            recv_sem=p_r.at[m, i, rep],
+            device_id=(section, place, other if rep else r),
             device_id_type=MESH,
         )
 
@@ -122,18 +130,20 @@
         sides(lambda: halo_copy(m, c, 0).start(), lambda: halo_copy(m, c, 1).start())
 
     def send_p(k, m, section):
-        p_copy(k, m, section, 2).start()
-        sides(
-            lambda: p_copy(k, m, section, 0).start(),
-            lambda: p_copy(k, m, section, 1).start(),
-        )
+        p_copy(k, m, section, 2, 1).start()
+        for rep in (1, 0):
+            sides(
+                lambda: p_copy(k, m, section, 0, rep).start(),
+                lambda: p_copy(k, m, section, 1, rep).start(),
+            )
 
     def wait_sent_p(k, m, section):
-        p_copy(k, m, section, 2).wait_send()
-        sides(
-            lambda: p_copy(k, m, section, 0).wait_send(),
-            lambda: p_copy(k, m, section, 1).wait_send(),
-        )
+        p_copy(k, m, section, 2, 1).wait_send()
+        for rep in (1, 0):
+            sides(
+                lambda: p_copy(k, m, section, 0, rep).wait_send(),
+                lambda: p_copy(k, m, section, 1, rep).wait_send(),
+            )
 
     def squares(m, rows, heads_of):
         total = None
@@ -147,12 +157,12 @@
     @pl.when(jnp.logical_not(has_left))
     def _():
         hid[:, pl.ds(own, half), :] = jnp.zeros((micro, half, width), BF16)
-        pin[:, pl.ds(own, half), :] = jnp.zeros((micro, half, HEAD), F32)
+        pin[:, :, pl.ds(own, half), :] = jnp.zeros((2, micro, half, HEAD), F32)
 
     @pl.when(jnp.logical_not(has_right))
     def _():
         hid[:, pl.ds(own + half, half), :] = jnp.zeros((micro, half, width), BF16)
-        pin[:, pl.ds(own + half, half), :] = jnp.zeros((micro, half, HEAD), F32)
+        pin[:, :, pl.ds(own + half, half), :] = jnp.zeros((2, micro, half, HEAD), F32)
 
     sig_copy.wait()
 
@@ -167,7 +177,7 @@
             pout[0, m] = partial
 
     beside = has_left.astype(jnp.int32) + has_right.astype(jnp.int32)
-    receivers = beside + jnp.where(last, 0, 2 + beside) + jnp.where(first, 1 + beside, 0)
+    receivers = beside + jnp.where(last, 0, 2 + 2 * beside) + jnp.where(first, 1 + beside, 0)
     pl.semaphore_wait(barrier, receivers)
 
     @pl.when(first)
@@ -205,40 +215,51 @@
     w_copy.wait()
     scale = math.log2(math.e) / math.sqrt(HEAD)
 
-    def inverse(m, rows):
-        total = jnp.sum(squares(m, rows, every) + pin[m, rows], axis=-1, keepdims=True)
+    def inverse(total):
+        total = jnp.sum(total, axis=-1, keepdims=True)
         return jnp.broadcast_to(lax.rsqrt(total / (HEADS * HEAD) + 1e-06), (own, HEAD))
 
     def normed(m, rows, h, inv):
         x = hid[m, rows, h * HEAD : (h + 1) * HEAD]
         return (x.astype(F32) * inv).astype(BF16)
 
+    @pl.when(jnp.logical_not(first))
+    def _():
+        for c in range(chunks):
+            own_copy(0, c).wait_recv()
+            forward_halo(0, c)
+
+    near = pl.ds(0, own)
+    beyond = pl.ds(own, own)
+
     @pl.loop(0, micro)
     def _(m):
-        @pl.when(jnp.logical_not(first))
-        def _():
-            for c in range(chunks):
-                own_copy(m, c).wait_recv()
-                forward_halo(m, c)
-
-        p_copy(1, m, following, 2).wait_recv()
-        inv = inverse(m, pl.ds(0, own))
+        mine = squares(m, near, every)
+        p_copy(1, m, following, 2, 1).wait_recv()
+        inv = inverse(mine + pin[1, m, near])
         for h in every:
-            x = normed(m, pl.ds(0, own), h, inv)
+            x = normed(m, near, h, inv)
             qkv[h] = jnp.dot(x, w[h], preferred_element_type=F32).astype(BF16)
-
-        def arrived(side):
-            p_copy(1, m, following, side).wait_recv()
-            for c in range(chunks):
-                halo_copy(m, c, side).wait_recv()
-
-        sides(lambda: arrived(1), lambda: arrived(0))
-        inv = inverse(m, pl.ds(own, own))
-        for h in every:
-            x = normed(m, pl.ds(own, own), h, inv)
-            halo_kv[h] = jnp.dot(x, w[h, :, HEAD:], preferred_element_type=F32).astype(BF16)
+        for rep in (1, 0):
+            sides(
+                lambda: p_copy(1, m, following, 1, rep).wait_recv(),
+                lambda: p_copy(1, m, following, 0, rep).wait_recv(),
+            )
+        inv = inverse(pin[0, m, beyond] + pin[1, m, beyond])
         sent = jnp.zeros((own, HEAD), F32)
         for c in range(chunks):
+            @pl.when(jnp.logical_not(first) & (m + 1 < micro))
+            def _():
+                own_copy(m + 1, c).wait_recv()
+                forward_halo(m + 1, c)
+
+            sides(
+                lambda: halo_copy(m, c, 1).wait_recv(),
+                lambda: halo_copy(m, c, 0).wait_recv(),
+            )
+            for h in range(c * GROUP, (c + 1) * GROUP):
+                x = normed(m, beyond, h, inv)
+                halo_kv[h] = jnp.dot(x, w[h, :, HEAD:], preferred_element_type=F32).astype(BF16)
             queries, keys, values = [], [], []
             blank = jnp.zeros((own, HEAD), BF16)
             for i in range(GROUP):
@@ -326,7 +347,7 @@
             pltpu.SMEM(record_pad.shape, jnp.int32),
             pltpu.VMEM((heads, own, 3 * HEAD), BF16),
             pltpu.VMEM((heads, own, 2 * HEAD), BF16),
-            pltpu.VMEM((micro, 2 * own, HEAD), F32),
+            pltpu.VMEM((2, micro, 2 * own, HEAD), F32),
             pltpu.VMEM((2, micro, own, HEAD), F32),
             pltpu.VMEM((micro, 2 * own, 4 * own), F32),
             pltpu.VMEM((micro, own, 4 * own), F32),
@@ -335,8 +356,8 @@
             dma((micro, chunks)),
             dma((micro, chunks, 2)),
             dma((micro, chunks, 2)),
-            dma((2, micro, 3)),
-            dma((micro, 3)),
+            dma((2, micro, 3, 2)),
+            dma((micro, 3, 2)),
         ],
         compiler_params=pltpu.CompilerParams(
             collective_id=0, has_side_effects=True, vmem_limit_bytes=40 * 2**20

time: 49.2 us -> 49.2 us (level)
  no operation moved by 1% of the time
where the time goes in v2:
time: 49.2 us; the launch traced here: 48.9 us
  Pallas kernels  48.1 us (98%)
  local copies, waits for them, and re-layouts  0.8 us (2%)
    pallas_call x1, Pallas kernels, body(): pl.pallas_call(kernel, name='relay', out_shape=jax.ShapeDtypeStruct((micr...  48.1 us

profile of v2, /device:TPU:7, one launch (start us, length us, event | category | flops | bytes accessed | tf_op | source)
XLA Modules:
  0.0 48.9 jit_solution(12476379586546802790)
XLA Ops:
  0.0 48.1 %relay.1 = bf16[2,32,2048]{2,1,0:T(8,128)(2,1)S(1)} custom-call(bf16[2,8,4,2048]{3,2,1,0:T(4,128)(2,1)} %sig_hbm.1, bf16[16,128,384]{2,1,0:T(8,128)(2,1)} %bitcast.1, s32[2,4]{1,0:T(2,128)} %start_hbm.1, s32[2,4]{1,0:T(2,128)} %pad_hbm.1), custom_call_target="tpu_custom_call" | custom-call | tf_op jit(solution)/shard_map/relay/pallas_call | solution.py:336
  48.1 0.8 %reshape.3 = bf16[1,2,8,4,2048]{4,3,2,1,0:T(4,128)(2,1)} reshape(bf16[2,32,2048]{2,1,0:T(8,128)(2,1)S(1)} %relay.1) | data formatting | bytes 524288 | tf_op jit(solution)/shard_map/reshape | solution.py:366

commit v3 on v2

v3 whole, which is shorter than its diff:
```python
import math

import jax
import jax.numpy as jnp
from jax import lax
from jax.experimental import pallas as pl
from jax.experimental.pallas import tpu as pltpu
from jax.sharding import PartitionSpec as P

HEADS = 32
HEAD = 128
REACH = 4
MESH = pl.DeviceIdType.MESH
F32 = jnp.float32
BF16 = jnp.bfloat16
GROUP = 4
MASKED = -1e30


def kernel(
    sig_hbm, w_hbm, start_hbm, pad_hbm, out,
    sig, hid, w, start, pad, qkv, halo_kv, pin, pout, res, bias_t, bias_s,
    in_sem, own_s, own_r, halo_s, halo_r, p_s, p_r, seed_s, seed_r, seed_h, end_s, end_r, ready,
):
    micro, own, width = out.shape
    heads = width // HEAD
    chunks = heads // GROUP
    half = own // 2
    sections = lax.axis_size("section")
    count = lax.axis_size("seq")
    s = lax.axis_index("section")
    j = lax.axis_index("seq")
    r = lax.axis_index("rep")
    other = 1 - r
    following = lax.rem(s + 1, sections)
    before = jnp.maximum(s - 1, 0)
    first = s == 0
    last = s == sections - 1

    late = first & (j == 0) & (r == 0)
    helper = first & (j == 1) & (r == 0)
    donor = (s == 1) & (j == 0) & (r == 0)
    active = jnp.logical_not(late)

    def number(flag):
        return flag.astype(jnp.int32)

    def sides(to_left, to_right, tile=0):
        at = j - tile

        @pl.when(at > 0)
        def _():
            to_left()

        @pl.when(at < count - 1)
        def _():
            to_right()

    w_copy = pltpu.make_async_copy(w_hbm, w, in_sem.at[0])
    sig_copy = pltpu.make_async_copy(sig_hbm, sig, in_sem.at[1])
    start_copy = pltpu.make_async_copy(start_hbm, start, in_sem.at[2])
    pad_copy = pltpu.make_async_copy(pad_hbm, pad, in_sem.at[3])
    sig_copy.start()
    w_copy.start()
    start_copy.start()
    pad_copy.start()

    barrier = pltpu.get_barrier_semaphore()

    def signal(device):
        pl.semaphore_signal(barrier, inc=1, device_id=device, device_id_type=MESH)

    def greet(section, place, rep):
        is_late = (section == 0) & (place == 0) & (rep == 0)

        @pl.when(jnp.logical_not(is_late & (s == 1)))
        def _():
            signal((section + number(is_late), place, rep))

    left = jnp.maximum(j - 1, 0)
    right = jnp.minimum(j + 1, count - 1)
    has_left = j > 0
    has_right = j < count - 1

    @pl.when(active)
    def _():
        greet(before, j, other)
        sides(lambda: greet(s, left, r), lambda: greet(s, right, r))
        sides(lambda: greet(before, left, other), lambda: greet(before, right, other))

        @pl.when(jnp.logical_not(first))
        def _():
            greet(before, j, r)
            sides(lambda: greet(before, left, r), lambda: greet(before, right, r))

    @pl.when(helper)
    def _():
        signal((s, left, r))

    def lanes(c):
        return pl.ds(c * GROUP * HEAD, GROUP * HEAD)

    def own_copy(t, m, c):
        return pltpu.make_async_remote_copy(
            src_ref=res.at[t, m, :, lanes(c)],
            dst_ref=hid.at[0, m, pl.ds(0, own), lanes(c)],
            send_sem=own_s.at[t, m, c],
            recv_sem=own_r.at[m, c],
            device_id=(following, j - t, r),
            device_id_type=MESH,
        )

    def halo_copy(m, c, side):
        return pltpu.make_async_remote_copy(
            src_ref=hid.at[0, m, pl.ds(side * half, half), lanes(c)],
            dst_ref=hid.at[0, m, pl.ds(own + (1 - side) * half, half), lanes(c)],
            send_sem=halo_s.at[m, c, side],
            recv_sem=halo_r.at[m, c, side],
            device_id=(s, right if side else left, r),
            device_id_type=MESH,
        )

    def seed_copy(m):
        return pltpu.make_async_remote_copy(
            src_ref=res.at[1, m],
            dst_ref=hid.at[1, m, pl.ds(0, own)],
            send_sem=seed_s.at[m],
            recv_sem=seed_r.at[m],
            device_id=(before, right, r),
            device_id_type=MESH,
        )

    def seed_halo_copy(m, c):
        return pltpu.make_async_remote_copy(
            src_ref=res.at[1, m, pl.ds(half, half), lanes(c)],
            dst_ref=hid.at[0, m, pl.ds(own, half), lanes(c)],
            send_sem=seed_h.at[m, c],
            recv_sem=halo_r.at[m, c, 1],
            device_id=(before, right, r),
            device_id_type=MESH,
        )

    def end_copy(m):
        return pltpu.make_async_remote_copy(
            src_ref=res.at[1, m],
            dst_ref=out.at[m],
            send_sem=end_s.at[m],
            recv_sem=end_r.at[m],
            device_id=(s, left, r),
            device_id_type=MESH,
        )

    def rows_of(i):
        return (
            (pl.ds(0, half), pl.ds(own + half, half)),
            (pl.ds(half, half), pl.ds(own, half)),
            (pl.ds(0, own), pl.ds(0, own)),
        )[i]

    def p_copy(k, t, m, section, i, rep):
        src, dst = rows_of(i)
        at = j - t
        place = (jnp.maximum(at - 1, 0), jnp.minimum(at + 1, count - 1), at)[i]
        to = other if rep else r
        moved = number((section == 0) & (place == 0) & (to == 0))
        return pltpu.make_async_remote_copy(
            src_ref=pout.at[k, t, m, src],
            dst_ref=pin.at[moved, rep, m, dst],
            send_sem=p_s.at[k, t, m, i, rep],
            recv_sem=p_r.at[moved, m, i, rep],
            device_id=(section, place + moved, to),
            device_id_type=MESH,
        )

    def p_arrived(t, m, i, rep):
        src, dst = rows_of(i)
        pltpu.make_async_remote_copy(
            src_ref=pout.at[0, 0, m, src],
            dst_ref=pin.at[t, rep, m, dst],
            send_sem=p_s.at[0, 0, m, i, rep],
            recv_sem=p_r.at[t, m, i, rep],
            device_id=(s, j, other),
            device_id_type=MESH,
        ).wait_recv()

    def forward_halo(m, c):
        @pl.when(jnp.logical_not(helper))
        def _():
            sides(lambda: halo_copy(m, c, 0).start(), lambda: None)

        sides(lambda: None, lambda: halo_copy(m, c, 1).start())

    def each_p(k, t, m, section, act):
        act(p_copy(k, t, m, section, 2, 1))
        sides(
            lambda: act(p_copy(k, t, m, section, 0, 1)),
            lambda: act(p_copy(k, t, m, section, 1, 1)),
            t,
        )

        def to_left():
            if k:
                act(p_copy(k, t, m, section, 0, 0))
            else:
                @pl.when(jnp.logical_not(helper))
                def _():
                    act(p_copy(k, t, m, section, 0, 0))

        sides(to_left, lambda: act(p_copy(k, t, m, section, 1, 0)), t)

    def squares(t, m, rows, heads_of):
        total = None
        for h in heads_of:
            x = hid[t, m, rows, h * HEAD : (h + 1) * HEAD].astype(F32)
            total = x * x if total is None else total + x * x
        return total

    every = range(heads)

    def clear(t, rows):
        hid[t, :, rows, :] = jnp.zeros((micro, half, width), BF16)
        pin[t, :, :, rows, :] = jnp.zeros((2, micro, half, HEAD), F32)

    before_own, after_own = pl.ds(own, half), pl.ds(own + half, half)
    sides_missing = (jnp.logical_not(has_left), jnp.logical_not(has_right))

    @pl.when(sides_missing[0] & active)
    def _():
        clear(0, before_own)

    @pl.when(sides_missing[1])
    def _():
        clear(0, after_own)

    @pl.when(helper)
    def _():
        clear(1, before_own)

    sig_copy.wait()

    def relaid(store):
        for m in range(micro):
            partial = jnp.zeros((own, HEAD), F32)
            for h in every:
                cols = slice(h * HEAD, (h + 1) * HEAD)
                x = sig[m, :, :, cols].astype(F32).reshape(own, HEAD)
                partial = partial + x * x
                store(m, cols, x.astype(BF16))
            pout[0, 0, m] = partial

    @pl.when(first & active)
    def _():
        def store(m, cols, x):
            hid[0, m, pl.ds(0, own), cols] = x

        relaid(store)

    @pl.when(donor)
    def _():
        def store(m, cols, x):
            res[1, m, :, cols] = x

        relaid(store)

    @pl.when(helper)
    def _():
        for m in range(micro):
            hid[1, m, after_own, :] = hid[0, m, pl.ds(0, half), :]
            pin[1, 0, m, after_own] = pout[0, 0, m, pl.ds(0, half)]

    beside = number(has_left) + number(has_right)
    receivers = beside + jnp.where(last, 0, 2 + 2 * beside) + jnp.where(first, 1 + beside, 0)
    fewer = number(helper) + number(first & (j <= 1) & (r == 1))
    receivers = receivers - fewer + 3 * number(donor)
    pl.semaphore_wait(barrier, jnp.where(late, 1, receivers))

    @pl.when(late)
    def _():
        pl.semaphore_signal(ready, inc=1, device_id=(s, right, r), device_id_type=MESH)

    @pl.when((first & active) | donor)
    def _():
        for m in range(micro):
            each_p(0, 0, m, 0, lambda copy: copy.start())

    @pl.when(first & active)
    def _():
        for m in range(micro):
            for c in range(chunks):
                forward_halo(m, c)

    @pl.when(donor)
    def _():
        for m in range(micro):
            for c in range(chunks):
                seed_halo_copy(m, c).start()
            seed_copy(m).start()

    start_copy.wait()
    pad_copy.wait()

    row = lax.broadcasted_iota(jnp.int32, (2 * own, 4 * own), 0)
    col = lax.broadcasted_iota(jnp.int32, (2 * own, 4 * own), 1) & (own - 1)
    key_time = (row >> 2) - jnp.where(row < own, 0, jnp.where(row < own + half, 12, 4))
    key_station = row & 3
    query_time = col >> 2
    query_station = col & 3
    total_steps = count * (own // 4)
    same_time = key_time == query_time
    same_station = key_station == query_station
    close = jnp.abs(key_time - query_time) <= REACH

    def set_bias(t):
        step = (j - t) * (own // 4) + key_time
        for m in range(micro):
            begin = jnp.zeros_like(row)
            end = jnp.zeros_like(row)
            for z in range(4):
                begin = jnp.where(key_station == z, start[m, z], begin)
                end = jnp.where(key_station == z, total_steps - pad[m, z], end)
            valid = (step >= begin) & (step < end)
            keep = same_station & close & (valid | same_time)
            bias_t[t, m] = jnp.where(keep, 0.0, MASKED)
            keep = same_time & (valid | same_station)
            bias_s[t, m] = jnp.where(keep, 0.0, MASKED)[:own]

    set_bias(0)

    @pl.when(helper)
    def _():
        set_bias(1)

    w_copy.wait()
    scale = math.log2(math.e) / math.sqrt(HEAD)

    def inverse(total):
        total = jnp.sum(total, axis=-1, keepdims=True)
        return jnp.broadcast_to(lax.rsqrt(total / (HEADS * HEAD) + 1e-06), (own, HEAD))

    def normed(t, m, rows, h, inv):
        x = hid[t, m, rows, h * HEAD : (h + 1) * HEAD]
        return (x.astype(F32) * inv).astype(BF16)

    @pl.when(jnp.logical_not(first))
    def _():
        for c in range(chunks):
            own_copy(0, 0, c).wait_recv()
            forward_halo(0, c)

    near = pl.ds(0, own)
    beyond = pl.ds(own, own)

    tiles = 1 + number(helper)

    @pl.loop(0, jnp.where(late, 0, micro * tiles))
    def _(turn):
        m = turn // tiles
        t = turn % tiles

        @pl.when(t == 1)
        def _():
            seed_copy(m).wait_recv()

        mine = squares(t, m, near, every)
        p_arrived(t, m, 2, 1)
        inv = inverse(mine + pin[t, 1, m, near])
        for h in every:
            x = normed(t, m, near, h, inv)
            qkv[h] = jnp.dot(x, w[h], preferred_element_type=F32).astype(BF16)
        sides(lambda: p_arrived(t, m, 1, 1), lambda: p_arrived(t, m, 0, 1), t)

        @pl.when(t == 0)
        def _():
            sides(lambda: p_arrived(0, m, 1, 0), lambda: p_arrived(0, m, 0, 0))

        inv = inverse(pin[t, 0, m, beyond] + pin[t, 1, m, beyond])
        sent = jnp.zeros((own, HEAD), F32)
        for c in range(chunks):
            @pl.when(jnp.logical_not(first) & (m + 1 < micro))
            def _():
                own_copy(0, m + 1, c).wait_recv()
                forward_halo(m + 1, c)

            @pl.when(t == 0)
            def _():
                sides(
                    lambda: halo_copy(m, c, 1).wait_recv(),
                    lambda: halo_copy(m, c, 0).wait_recv(),
                )

            for h in range(c * GROUP, (c + 1) * GROUP):
                x = normed(t, m, beyond, h, inv)
                halo_kv[h] = jnp.dot(x, w[h, :, HEAD:], preferred_element_type=F32).astype(BF16)
            queries, keys, values = [], [], []
            blank = jnp.zeros((own, HEAD), BF16)
            for i in range(GROUP):
                h = c * GROUP + i
                q = qkv[h, :, :HEAD]
                queries.append(
                    jnp.concatenate([q if i == n else blank for n in range(GROUP)], axis=1)
                )
                k = qkv[h, :, HEAD : 2 * HEAD]
                keys.append(jnp.concatenate([k, halo_kv[h, :, :HEAD]], axis=0))
                v = qkv[h, :, 2 * HEAD :]
                values.append(jnp.concatenate([v, halo_kv[h, :, HEAD:], v], axis=0))
            scores = lax.dot_general(
                jnp.concatenate(keys, axis=1),
                jnp.concatenate(queries, axis=0),
                (((1,), (1,)), ((), ())),
                preferred_element_type=F32,
            ) * scale
            along = scores + bias_t[t, m]
            along = jnp.exp2(along - jnp.max(along, axis=0, keepdims=True))
            along = along * (1.0 / jnp.sum(along, axis=0, keepdims=True))
            across = scores[:own] + bias_s[t, m]
            across = jnp.exp2(across - jnp.max(across, axis=0, keepdims=True))
            across = across * (1.0 / jnp.sum(across, axis=0, keepdims=True))
            mix = jnp.transpose(jnp.concatenate([along, across], axis=0)).astype(BF16)
            for i in range(GROUP):
                h = c * GROUP + i
                update = jnp.dot(
                    mix[i * own : (i + 1) * own], values[i], preferred_element_type=F32
                )
                x = hid[t, m, pl.ds(0, own), h * HEAD : (h + 1) * HEAD].astype(F32)
                y = (x + update).astype(BF16)
                res[t, m, :, h * HEAD : (h + 1) * HEAD] = y
                y = y.astype(F32)
                sent = sent + y * y

            @pl.when(jnp.logical_not(last))
            def _():
                own_copy(t, m, c).start()

        @pl.when(jnp.logical_not(last))
        def _():
            pout[1, t, m] = sent
            each_p(1, t, m, following, lambda copy: copy.start())

    @pl.when(active)
    def _():
        out[...] = res[0]

        @pl.when(jnp.logical_not(helper))
        def _():
            sides(
                lambda: [halo_copy(m, c, 0).wait_send() for m in range(micro) for c in range(chunks)],
                lambda: None,
            )

        sides(
            lambda: None,
            lambda: [halo_copy(m, c, 1).wait_send() for m in range(micro) for c in range(chunks)],
        )

    def wait_sent(t):
        for m in range(micro):
            for c in range(chunks):
                own_copy(t, m, c).wait_send()
            each_p(1, t, m, following, lambda copy: copy.wait_send())

    @pl.when(active & jnp.logical_not(last))
    def _():
        wait_sent(0)

    @pl.when((first & active) | donor)
    def _():
        for m in range(micro):
            each_p(0, 0, m, 0, lambda copy: copy.wait_send())

    @pl.when(donor)
    def _():
        for m in range(micro):
            for c in range(chunks):
                seed_halo_copy(m, c).wait_send()
            seed_copy(m).wait_send()

    @pl.when(helper)
    def _():
        wait_sent(1)
        pl.semaphore_wait(ready, 1)
        for m in range(micro):
            end_copy(m).start()
        for m in range(micro):
            end_copy(m).wait_send()

    @pl.when(late)
    def _():
        for m in range(micro):
            end_copy(m).wait_recv()


def body(signal, head_proj, record_start, record_pad):
    micro, times, stations, width = signal.shape
    own = times * stations
    heads = width // HEAD
    chunks = heads // GROUP
    dma = pltpu.SemaphoreType.DMA
    vmem = pl.BlockSpec(memory_space=pltpu.VMEM)
    hbm = pl.BlockSpec(memory_space=pltpu.HBM)
    result = pl.pallas_call(
        kernel,
        name="relay",
        out_shape=jax.ShapeDtypeStruct((micro, own, width), BF16),
        in_specs=[hbm] * 4,
        out_specs=vmem,
        scratch_shapes=[
            pltpu.VMEM(signal.shape, BF16),
            pltpu.VMEM((2, micro, 2 * own, width), BF16),
            pltpu.VMEM((heads, HEAD, 3 * HEAD), BF16),
            pltpu.SMEM(record_start.shape, jnp.int32),
            pltpu.SMEM(record_pad.shape, jnp.int32),
            pltpu.VMEM((heads, own, 3 * HEAD), BF16),
            pltpu.VMEM((heads, own, 2 * HEAD), BF16),
            pltpu.VMEM((2, 2, micro, 2 * own, HEAD), F32),
            pltpu.VMEM((2, 2, micro, own, HEAD), F32),
            pltpu.VMEM((2, micro, own, width), BF16),
            pltpu.VMEM((2, micro, 2 * own, 4 * own), F32),
            pltpu.VMEM((2, micro, own, 4 * own), F32),
            dma((4,)),
            dma((2, micro, chunks)),
            dma((micro, chunks)),
            dma((micro, chunks, 2)),
            dma((micro, chunks, 2)),
            dma((2, 2, micro, 3, 2)),
            dma((2, micro, 3, 2)),
            dma((micro,)),
            dma((micro,)),
            dma((micro, chunks)),
            dma((micro,)),
            dma((micro,)),
            pltpu.SemaphoreType.REGULAR,
        ],
        compiler_params=pltpu.CompilerParams(
            collective_id=0, has_side_effects=True, vmem_limit_bytes=40 * 2**20
        ),
    )(*[pltpu.with_memory_space_constraint(x, pltpu.HBM) for x in (signal, head_proj[0], record_start, record_pad)])
    return result.reshape(1, micro, times, stations, width)


def solution(mesh):
    return jax.shard_map(
        body,
        mesh=mesh,
        in_specs=(P(None, "seq", None, "rep"), P("section", "rep", None, None), P(), P()),
        out_specs=P("section", None, "seq", None, "rep"),
        check_vma=False,
    )
```

time: 49.2 us -> 43.1 us (0.88)
  Pallas kernels: 48.1 us -> 41.9 us
    pallas_call x1, Pallas kernels: 48.1 us -> 41.9 us  [body(): pl.pallas_call(kernel, name='relay', out_shape=jax.ShapeDtypeStruct((micr...]
where the time goes in v3:
time: 43.1 us; the launch traced here: 42.7 us
  Pallas kernels  41.9 us (97%)
  local copies, waits for them, and re-layouts  0.8 us (2%)
    pallas_call x1, Pallas kernels, body(): pl.pallas_call(kernel, name='relay', out_shape=jax.ShapeDtypeStruct((micr...  41.9 us

profile of v3, /device:TPU:7, one launch (start us, length us, event | category | flops | bytes accessed | tf_op | source)
XLA Modules:
  0.0 42.7 jit_solution(3342739047355000594)
XLA Ops:
  0.0 41.9 %relay.1 = bf16[2,32,2048]{2,1,0:T(8,128)(2,1)S(1)} custom-call(bf16[2,8,4,2048]{3,2,1,0:T(4,128)(2,1)} %sig_hbm.1, bf16[16,128,384]{2,1,0:T(8,128)(2,1)} %bitcast.1, s32[2,4]{1,0:T(2,128)} %start_hbm.1, s32[2,4]{1,0:T(2,128)} %pad_hbm.1), custom_call_target="tpu_custom_call" | custom-call | tf_op jit(solution)/shard_map/relay/pallas_call | solution.py:500
  41.9 0.8 %reshape.3 = bf16[1,2,8,4,2048]{4,3,2,1,0:T(4,128)(2,1)} reshape(bf16[2,32,2048]{2,1,0:T(8,128)(2,1)S(1)} %relay.1) | data formatting | bytes 524288 | tf_op jit(solution)/shard_map/reshape | solution.py:537

commit v4 on v3

--- a/solution.py
+++ b/solution.py
@@ -14,12 +14,13 @@
 F32 = jnp.float32
 BF16 = jnp.bfloat16
 GROUP = 4
+BLOCKS = ((0,), (1,), (2,), (3,))
 MASKED = -1e30
 
 
 def kernel(
     sig_hbm, w_hbm, start_hbm, pad_hbm, out,
-    sig, hid, w, start, pad, qkv, halo_kv, pin, pout, res, bias_t, bias_s,
+    sig, hid, w, start, pad, pin, pout, res, bias_t, bias_s,
     in_sem, own_s, own_r, halo_s, halo_r, p_s, p_r, seed_s, seed_r, seed_h, end_s, end_r, ready,
 ):
     micro, own, width = out.shape
@@ -150,22 +151,14 @@
             device_id_type=MESH,
         )
 
-    def rows_of(i):
-        return (
-            (pl.ds(0, half), pl.ds(own + half, half)),
-            (pl.ds(half, half), pl.ds(own, half)),
-            (pl.ds(0, own), pl.ds(0, own)),
-        )[i]
-
     def p_copy(k, t, m, section, i, rep):
-        src, dst = rows_of(i)
         at = j - t
         place = (jnp.maximum(at - 1, 0), jnp.minimum(at + 1, count - 1), at)[i]
         to = other if rep else r
         moved = number((section == 0) & (place == 0) & (to == 0))
         return pltpu.make_async_remote_copy(
-            src_ref=pout.at[k, t, m, src],
-            dst_ref=pin.at[moved, rep, m, dst],
+            src_ref=pout.at[k, t, m],
+            dst_ref=pin.at[moved, rep, m, i],
             send_sem=p_s.at[k, t, m, i, rep],
             recv_sem=p_r.at[moved, m, i, rep],
             device_id=(section, place + moved, to),
@@ -173,15 +166,33 @@
         )
 
     def p_arrived(t, m, i, rep):
-        src, dst = rows_of(i)
         pltpu.make_async_remote_copy(
-            src_ref=pout.at[0, 0, m, src],
-            dst_ref=pin.at[t, rep, m, dst],
+            src_ref=pout.at[0, 0, m],
+            dst_ref=pin.at[t, rep, m, i],
             send_sem=p_s.at[0, 0, m, i, rep],
             recv_sem=p_r.at[t, m, i, rep],
             device_id=(s, j, other),
             device_id_type=MESH,
         ).wait_recv()
+
+    lane = lax.broadcasted_iota(jnp.int32, (8, HEAD), 1)
+
+    def folded(p):
+        wide = lax.broadcasted_iota(jnp.int32, (16, HEAD), 1)
+        low, high = p[:16], p[16:]
+        p = jnp.where(wide < 64, low + pltpu.roll(low, 64, 1), high + pltpu.roll(high, 64, 1))
+        low, high = p[:8], p[8:]
+        return jnp.where(
+            (lane & 32) == 0, low + pltpu.roll(low, 96, 1), high + pltpu.roll(high, 32, 1)
+        )
+
+    def inverse(*parts):
+        total = [
+            jnp.sum(jnp.where((lane >> 5) == g, p, 0.0), axis=-1, keepdims=True)
+            for p, g in parts
+        ]
+        total = jnp.concatenate(total, axis=0)
+        return jnp.broadcast_to(lax.rsqrt(total / (HEADS * HEAD) + 1e-06), (own, HEAD))
 
     def forward_halo(m, c):
         @pl.when(jnp.logical_not(helper))
@@ -217,24 +228,24 @@
 
     every = range(heads)
 
-    def clear(t, rows):
+    def clear(t, rows, i):
         hid[t, :, rows, :] = jnp.zeros((micro, half, width), BF16)
-        pin[t, :, :, rows, :] = jnp.zeros((2, micro, half, HEAD), F32)
+        pin[t, :, :, i] = jnp.zeros((2, micro, 8, HEAD), F32)
 
     before_own, after_own = pl.ds(own, half), pl.ds(own + half, half)
     sides_missing = (jnp.logical_not(has_left), jnp.logical_not(has_right))
 
     @pl.when(sides_missing[0] & active)
     def _():
-        clear(0, before_own)
+        clear(0, before_own, 1)
 
     @pl.when(sides_missing[1])
     def _():
-        clear(0, after_own)
+        clear(0, after_own, 0)
 
     @pl.when(helper)
     def _():
-        clear(1, before_own)
+        clear(1, before_own, 1)
 
     sig_copy.wait()
 
@@ -246,7 +257,7 @@
                 x = sig[m, :, :, cols].astype(F32).reshape(own, HEAD)
                 partial = partial + x * x
                 store(m, cols, x.astype(BF16))
-            pout[0, 0, m] = partial
+            pout[0, 0, m] = folded(partial)
 
     @pl.when(first & active)
     def _():
@@ -266,7 +277,7 @@
     def _():
         for m in range(micro):
             hid[1, m, after_own, :] = hid[0, m, pl.ds(0, half), :]
-            pin[1, 0, m, after_own] = pout[0, 0, m, pl.ds(0, half)]
+            pin[1, 0, m, 0] = pout[0, 0, m]
 
     beside = number(has_left) + number(has_right)
     receivers = beside + jnp.where(last, 0, 2 + 2 * beside) + jnp.where(first, 1 + beside, 0)
@@ -333,10 +344,6 @@
     w_copy.wait()
     scale = math.log2(math.e) / math.sqrt(HEAD)
 
-    def inverse(total):
-        total = jnp.sum(total, axis=-1, keepdims=True)
-        return jnp.broadcast_to(lax.rsqrt(total / (HEADS * HEAD) + 1e-06), (own, HEAD))
-
     def normed(t, m, rows, h, inv):
         x = hid[t, m, rows, h * HEAD : (h + 1) * HEAD]
         return (x.astype(F32) * inv).astype(BF16)
@@ -349,6 +356,48 @@
 
     near = pl.ds(0, own)
     beyond = pl.ds(own, own)
+
+    def attend(t, m, c, inv_near, inv_beyond, sent):
+        queries, keys, values = [], [], []
+        blank = jnp.zeros((own, HEAD), BF16)
+        for i in range(GROUP):
+            h = c * GROUP + i
+            x = normed(t, m, near, h, inv_near)
+            qkv = jnp.dot(x, w[h], preferred_element_type=F32).astype(BF16)
+            x = normed(t, m, beyond, h, inv_beyond)
+            kv = jnp.dot(x, w[h, :, HEAD:], preferred_element_type=F32).astype(BF16)
+            q = qkv[:, :HEAD]
+            queries.append(
+                jnp.concatenate([q if i == n else blank for n in range(GROUP)], axis=1)
+            )
+            k = qkv[:, HEAD : 2 * HEAD]
+            keys.append(jnp.concatenate([k, kv[:, :HEAD]], axis=0))
+            v = qkv[:, 2 * HEAD :]
+            values.append(jnp.concatenate([v, kv[:, HEAD:], v], axis=0))
+        scores = lax.dot_general(
+            jnp.concatenate(keys, axis=1),
+            jnp.concatenate(queries, axis=0),
+            (((1,), (1,)), ((), ())),
+            preferred_element_type=F32,
+        ) * scale
+        along = scores + bias_t[t, m]
+        along = jnp.exp2(along - jnp.max(along, axis=0, keepdims=True))
+        along = along * (1.0 / jnp.sum(along, axis=0, keepdims=True))
+        across = scores[:own] + bias_s[t, m]
+        across = jnp.exp2(across - jnp.max(across, axis=0, keepdims=True))
+        across = across * (1.0 / jnp.sum(across, axis=0, keepdims=True))
+        mix = jnp.transpose(jnp.concatenate([along, across], axis=0)).astype(BF16)
+        for i in range(GROUP):
+            h = c * GROUP + i
+            update = jnp.dot(
+                mix[i * own : (i + 1) * own], values[i], preferred_element_type=F32
+            )
+            x = hid[t, m, pl.ds(0, own), h * HEAD : (h + 1) * HEAD].astype(F32)
+            y = (x + update).astype(BF16)
+            res[t, m, :, h * HEAD : (h + 1) * HEAD] = y
+            y = y.astype(F32)
+            sent = sent + y * y
+        return sent
 
     tiles = 1 + number(helper)
 
@@ -361,79 +410,45 @@
         def _():
             seed_copy(m).wait_recv()
 
-        mine = squares(t, m, near, every)
+        mine = folded(squares(t, m, near, every))
         p_arrived(t, m, 2, 1)
-        inv = inverse(mine + pin[t, 1, m, near])
-        for h in every:
-            x = normed(t, m, near, h, inv)
-            qkv[h] = jnp.dot(x, w[h], preferred_element_type=F32).astype(BF16)
         sides(lambda: p_arrived(t, m, 1, 1), lambda: p_arrived(t, m, 0, 1), t)
 
         @pl.when(t == 0)
         def _():
             sides(lambda: p_arrived(0, m, 1, 0), lambda: p_arrived(0, m, 0, 0))
 
-        inv = inverse(pin[t, 0, m, beyond] + pin[t, 1, m, beyond])
+        mine = mine + pin[t, 1, m, 2]
+        inv_near = inverse((mine, 0), (mine, 1), (mine, 2), (mine, 3))
+        lower = pin[t, 0, m, 1] + pin[t, 1, m, 1]
+        upper = pin[t, 0, m, 0] + pin[t, 1, m, 0]
+        inv_beyond = inverse((lower, 2), (lower, 3), (upper, 0), (upper, 1))
         sent = jnp.zeros((own, HEAD), F32)
-        for c in range(chunks):
-            @pl.when(jnp.logical_not(first) & (m + 1 < micro))
-            def _():
-                own_copy(0, m + 1, c).wait_recv()
-                forward_halo(m + 1, c)
+        for block in BLOCKS:
+            for c in block:
+                @pl.when(jnp.logical_not(first) & (m + 1 < micro))
+                def _():
+                    own_copy(0, m + 1, c).wait_recv()
+                    forward_halo(m + 1, c)
 
             @pl.when(t == 0)
             def _():
                 sides(
-                    lambda: halo_copy(m, c, 1).wait_recv(),
-                    lambda: halo_copy(m, c, 0).wait_recv(),
+                    lambda: [halo_copy(m, c, 1).wait_recv() for c in block],
+                    lambda: [halo_copy(m, c, 0).wait_recv() for c in block],
                 )
 
-            for h in range(c * GROUP, (c + 1) * GROUP):
-                x = normed(t, m, beyond, h, inv)
-                halo_kv[h] = jnp.dot(x, w[h, :, HEAD:], preferred_element_type=F32).astype(BF16)
-            queries, keys, values = [], [], []
-            blank = jnp.zeros((own, HEAD), BF16)
-            for i in range(GROUP):
-                h = c * GROUP + i
-                q = qkv[h, :, :HEAD]
-                queries.append(
-                    jnp.concatenate([q if i == n else blank for n in range(GROUP)], axis=1)
-                )
-                k = qkv[h, :, HEAD : 2 * HEAD]
-                keys.append(jnp.concatenate([k, halo_kv[h, :, :HEAD]], axis=0))
-                v = qkv[h, :, 2 * HEAD :]
-                values.append(jnp.concatenate([v, halo_kv[h, :, HEAD:], v], axis=0))
-            scores = lax.dot_general(
-                jnp.concatenate(keys, axis=1),
-                jnp.concatenate(queries, axis=0),
-                (((1,), (1,)), ((), ())),
-                preferred_element_type=F32,
-            ) * scale
-            along = scores + bias_t[t, m]
-            along = jnp.exp2(along - jnp.max(along, axis=0, keepdims=True))
-            along = along * (1.0 / jnp.sum(along, axis=0, keepdims=True))
-            across = scores[:own] + bias_s[t, m]
-            across = jnp.exp2(across - jnp.max(across, axis=0, keepdims=True))
-            across = across * (1.0 / jnp.sum(across, axis=0, keepdims=True))
-            mix = jnp.transpose(jnp.concatenate([along, across], axis=0)).astype(BF16)
-            for i in range(GROUP):
-                h = c * GROUP + i
-                update = jnp.dot(
-                    mix[i * own : (i + 1) * own], values[i], preferred_element_type=F32
-                )
-                x = hid[t, m, pl.ds(0, own), h * HEAD : (h + 1) * HEAD].astype(F32)
-                y = (x + update).astype(BF16)
-                res[t, m, :, h * HEAD : (h + 1) * HEAD] = y
-                y = y.astype(F32)
-                sent = sent + y * y
+            for c in block:
+                sent = attend(t, m, c, inv_near, inv_beyond, sent)
 
             @pl.when(jnp.logical_not(last))
             def _():
-                own_copy(t, m, c).start()
+                for c in block:
+                    own_copy(t, m, c).start()
 
         @pl.when(jnp.logical_not(last))
         def _():
-            pout[1, t, m] = sent
+            pout[1, t, m] = folded(sent)
             each_p(1, t, m, following, lambda copy: copy.start())
 
     @pl.when(active)
@@ -509,10 +524,8 @@
             pltpu.VMEM((heads, HEAD, 3 * HEAD), BF16),
             pltpu.SMEM(record_start.shape, jnp.int32),
             pltpu.SMEM(record_pad.shape, jnp.int32),
-            pltpu.VMEM((heads, own, 3 * HEAD), BF16),
-            pltpu.VMEM((heads, own, 2 * HEAD), BF16),
-            pltpu.VMEM((2, 2, micro, 2 * own, HEAD), F32),
-            pltpu.VMEM((2, 2, micro, own, HEAD), F32),
+            pltpu.VMEM((2, 2, micro, 3, 8, HEAD), F32),
+            pltpu.VMEM((2, 2, micro, 8, HEAD), F32),
             pltpu.VMEM((2, micro, own, width), BF16),
             pltpu.VMEM((2, micro, 2 * own, 4 * own), F32),
             pltpu.VMEM((2, micro, own, 4 * own), F32),

time: 43.1 us -> 41.7 us (0.968)
  Pallas kernels: 41.9 us -> 40.7 us
    pallas_call x1, Pallas kernels: 41.9 us -> 40.7 us  [body(): pl.pallas_call(kernel, name='relay', out_shape=jax.ShapeDtypeStruct((micr...]
where the time goes in v4:
time: 41.7 us; the launch traced here: 41.5 us
  Pallas kernels  40.7 us (98%)
  local copies, waits for them, and re-layouts  0.8 us (2%)
    pallas_call x1, Pallas kernels, body(): pl.pallas_call(kernel, name='relay', out_shape=jax.ShapeDtypeStruct((micr...  40.7 us

profile of v4, /device:TPU:7, one launch (start us, length us, event | category | flops | bytes accessed | tf_op | source)
XLA Modules:
  0.0 41.5 jit_solution(14835052881318780622)
XLA Ops:
  0.0 40.7 %relay.1 = bf16[2,32,2048]{2,1,0:T(8,128)(2,1)S(1)} custom-call(bf16[2,8,4,2048]{3,2,1,0:T(4,128)(2,1)} %sig_hbm.1, bf16[16,128,384]{2,1,0:T(8,128)(2,1)} %bitcast.1, s32[2,4]{1,0:T(2,128)} %start_hbm.1, s32[2,4]{1,0:T(2,128)} %pad_hbm.1), custom_call_target="tpu_custom_call" | custom-call | tf_op jit(solution)/shard_map/relay/pallas_call | solution.py:515
  40.7 0.8 %reshape.3 = bf16[1,2,8,4,2048]{4,3,2,1,0:T(4,128)(2,1)} reshape(bf16[2,32,2048]{2,1,0:T(8,128)(2,1)S(1)} %relay.1) | data formatting | bytes 524288 | tf_op jit(solution)/shard_map/reshape | solution.py:550

commit v5 on v4

--- a/solution.py
+++ b/solution.py
@@ -14,13 +14,12 @@
 F32 = jnp.float32
 BF16 = jnp.bfloat16
 GROUP = 4
-BLOCKS = ((0,), (1,), (2,), (3,))
 MASKED = -1e30
 
 
 def kernel(
     sig_hbm, w_hbm, start_hbm, pad_hbm, out,
-    sig, hid, w, start, pad, pin, pout, res, bias_t, bias_s,
+    sig, hid, w, start, pad, qkv, halo_kv, pin, pout, res, bias_t, bias_s,
     in_sem, own_s, own_r, halo_s, halo_r, p_s, p_r, seed_s, seed_r, seed_h, end_s, end_r, ready,
 ):
     micro, own, width = out.shape
@@ -357,44 +356,49 @@
     near = pl.ds(0, own)
     beyond = pl.ds(own, own)
 
-    def attend(t, m, c, inv_near, inv_beyond, sent):
-        queries, keys, values = [], [], []
+    def project_near(t, m, inv):
+        for h in every:
+            x = normed(t, m, near, h, inv)
+            qkv[h] = jnp.dot(x, w[h], preferred_element_type=F32).astype(BF16)
+
+    def project_beyond(t, m, c, inv):
+        for h in range(c * GROUP, (c + 1) * GROUP):
+            x = normed(t, m, beyond, h, inv)
+            halo_kv[h] = jnp.dot(x, w[h, :, HEAD:], preferred_element_type=F32).astype(BF16)
+
+    def scores_of(c):
+        queries, keys = [], []
         blank = jnp.zeros((own, HEAD), BF16)
         for i in range(GROUP):
             h = c * GROUP + i
-            x = normed(t, m, near, h, inv_near)
-            qkv = jnp.dot(x, w[h], preferred_element_type=F32).astype(BF16)
-            x = normed(t, m, beyond, h, inv_beyond)
-            kv = jnp.dot(x, w[h, :, HEAD:], preferred_element_type=F32).astype(BF16)
-            q = qkv[:, :HEAD]
-            queries.append(
-                jnp.concatenate([q if i == n else blank for n in range(GROUP)], axis=1)
-            )
-            k = qkv[:, HEAD : 2 * HEAD]
-            keys.append(jnp.concatenate([k, kv[:, :HEAD]], axis=0))
-            v = qkv[:, 2 * HEAD :]
-            values.append(jnp.concatenate([v, kv[:, HEAD:], v], axis=0))
-        scores = lax.dot_general(
+            q = qkv[h, :, :HEAD]
+            queries.append(jnp.concatenate([q if i == n else blank for n in range(GROUP)], axis=1))
+            keys.append(jnp.concatenate([qkv[h, :, HEAD : 2 * HEAD], halo_kv[h, :, :HEAD]], axis=0))
+        return lax.dot_general(
             jnp.concatenate(keys, axis=1),
             jnp.concatenate(queries, axis=0),
             (((1,), (1,)), ((), ())),
             preferred_element_type=F32,
         ) * scale
+
+    def mixture(t, m, scores):
         along = scores + bias_t[t, m]
         along = jnp.exp2(along - jnp.max(along, axis=0, keepdims=True))
         along = along * (1.0 / jnp.sum(along, axis=0, keepdims=True))
         across = scores[:own] + bias_s[t, m]
         across = jnp.exp2(across - jnp.max(across, axis=0, keepdims=True))
         across = across * (1.0 / jnp.sum(across, axis=0, keepdims=True))
-        mix = jnp.transpose(jnp.concatenate([along, across], axis=0)).astype(BF16)
+        return jnp.transpose(jnp.concatenate([along, across], axis=0)).astype(BF16)
+
+    def update(t, m, c, mix, sent):
         for i in range(GROUP):
             h = c * GROUP + i
-            update = jnp.dot(
-                mix[i * own : (i + 1) * own], values[i], preferred_element_type=F32
-            )
-            x = hid[t, m, pl.ds(0, own), h * HEAD : (h + 1) * HEAD].astype(F32)
-            y = (x + update).astype(BF16)
-            res[t, m, :, h * HEAD : (h + 1) * HEAD] = y
+            cols = slice(h * HEAD, (h + 1) * HEAD)
+            v = qkv[h, :, 2 * HEAD :]
+            values = jnp.concatenate([v, halo_kv[h, :, HEAD:], v], axis=0)
+            change = jnp.dot(mix[i * own : (i + 1) * own], values, preferred_element_type=F32)
+            y = (hid[t, m, near, cols].astype(F32) + change).astype(BF16)
+            res[t, m, :, cols] = y
             y = y.astype(F32)
             sent = sent + y * y
         return sent
@@ -412,39 +416,47 @@
 
         mine = folded(squares(t, m, near, every))
         p_arrived(t, m, 2, 1)
+        mine = mine + pin[t, 1, m, 2]
+        project_near(t, m, inverse((mine, 0), (mine, 1), (mine, 2), (mine, 3)))
         sides(lambda: p_arrived(t, m, 1, 1), lambda: p_arrived(t, m, 0, 1), t)
 
         @pl.when(t == 0)
         def _():
             sides(lambda: p_arrived(0, m, 1, 0), lambda: p_arrived(0, m, 0, 0))
 
-        mine = mine + pin[t, 1, m, 2]
-        inv_near = inverse((mine, 0), (mine, 1), (mine, 2), (mine, 3))
         lower = pin[t, 0, m, 1] + pin[t, 1, m, 1]
         upper = pin[t, 0, m, 0] + pin[t, 1, m, 0]
-        inv_beyond = inverse((lower, 2), (lower, 3), (upper, 0), (upper, 1))
-        sent = jnp.zeros((own, HEAD), F32)
-        for block in BLOCKS:
-            for c in block:
-                @pl.when(jnp.logical_not(first) & (m + 1 < micro))
-                def _():
-                    own_copy(0, m + 1, c).wait_recv()
-                    forward_halo(m + 1, c)
+        inv = inverse((lower, 2), (lower, 3), (upper, 0), (upper, 1))
+
+        def gather(c):
+            @pl.when(jnp.logical_not(first) & (m + 1 < micro))
+            def _():
+                own_copy(0, m + 1, c).wait_recv()
+                forward_halo(m + 1, c)
 
             @pl.when(t == 0)
             def _():
                 sides(
-                    lambda: [halo_copy(m, c, 1).wait_recv() for c in block],
-                    lambda: [halo_copy(m, c, 0).wait_recv() for c in block],
+                    lambda: halo_copy(m, c, 1).wait_recv(),
+                    lambda: halo_copy(m, c, 0).wait_recv(),
                 )
 
-            for c in block:
-                sent = attend(t, m, c, inv_near, inv_beyond, sent)
+        sent = jnp.zeros((own, HEAD), F32)
+        gather(0)
+        project_beyond(t, m, 0, inv)
+        scores = scores_of(0)
+        for c in range(chunks):
+            later = None
+            if c + 1 < chunks:
+                gather(c + 1)
+                project_beyond(t, m, c + 1, inv)
+                later = scores_of(c + 1)
+            sent = update(t, m, c, mixture(t, m, scores), sent)
+            scores = later
 
             @pl.when(jnp.logical_not(last))
             def _():
-                for c in block:
-                    own_copy(t, m, c).start()
+                own_copy(t, m, c).start()
 
         @pl.when(jnp.logical_not(last))
         def _():
@@ -524,6 +536,8 @@
             pltpu.VMEM((heads, HEAD, 3 * HEAD), BF16),
             pltpu.SMEM(record_start.shape, jnp.int32),
             pltpu.SMEM(record_pad.shape, jnp.int32),
+            pltpu.VMEM((heads, own, 3 * HEAD), BF16),
+            pltpu.VMEM((heads, own, 2 * HEAD), BF16),
             pltpu.VMEM((2, 2, micro, 3, 8, HEAD), F32),
             pltpu.VMEM((2, 2, micro, 8, HEAD), F32),
             pltpu.VMEM((2, micro, own, width), BF16),

time: 41.7 us -> 40 us (0.959); the launches traced: 41.5 us -> 39.4 us
  Pallas kernels: 40.7 us -> 38.6 us
    pallas_call x1, Pallas kernels: 40.7 us -> 38.6 us  [body(): pl.pallas_call(kernel, name='relay', out_shape=jax.ShapeDtypeStruct((micr...]
where the time goes in v5:
time: 40 us; the launch traced here: 39.4 us
  Pallas kernels  38.6 us (96%)
  local copies, waits for them, and re-layouts  0.8 us (2%)
    pallas_call x1, Pallas kernels, body(): pl.pallas_call(kernel, name='relay', out_shape=jax.ShapeDtypeStruct((micr...  38.6 us
    reshape x1, local copies, waits for them, and re-layouts, body(): return result.reshape(1, micro, times, stations, width)  0.8 us

profile of v5, /device:TPU:7, one launch (start us, length us, event | category | flops | bytes accessed | tf_op | source)
XLA Modules:
  0.0 39.4 jit_solution(16903011038051898135)
XLA Ops:
  0.0 38.6 %relay.1 = bf16[2,32,2048]{2,1,0:T(8,128)(2,1)S(1)} custom-call(bf16[2,8,4,2048]{3,2,1,0:T(4,128)(2,1)} %sig_hbm.1, bf16[16,128,384]{2,1,0:T(8,128)(2,1)} %bitcast.1, s32[2,4]{1,0:T(2,128)} %start_hbm.1, s32[2,4]{1,0:T(2,128)} %pad_hbm.1), custom_call_target="tpu_custom_call" | custom-call | tf_op jit(solution)/shard_map/relay/pallas_call | solution.py:527
  38.6 0.8 %reshape.3 = bf16[1,2,8,4,2048]{4,3,2,1,0:T(4,128)(2,1)} reshape(bf16[2,32,2048]{2,1,0:T(8,128)(2,1)S(1)} %relay.1) | data formatting | bytes 524288 | tf_op jit(solution)/shard_map/reshape | solution.py:564

commit v6 on v5

--- a/solution.py
+++ b/solution.py
@@ -456,12 +456,10 @@
 
             @pl.when(jnp.logical_not(last))
             def _():
+                if c + 1 == chunks:
+                    pout[1, t, m] = folded(sent)
+                    each_p(1, t, m, following, lambda copy: copy.start())
                 own_copy(t, m, c).start()
-
-        @pl.when(jnp.logical_not(last))
-        def _():
-            pout[1, t, m] = folded(sent)
-            each_p(1, t, m, following, lambda copy: copy.start())
 
     @pl.when(active)
     def _():

time: 40 us -> 39.5 us (0.988)
  the two profiles are of different devices: /device:TPU:7 before, /device:TPU:111 now
where the time goes in v6:
time: 39.5 us; the launch traced here: 39.4 us
  Pallas kernels  38.5 us (97%)
  local copies, waits for them, and re-layouts  0.8 us (2%)
    pallas_call x1, Pallas kernels, body(): pl.pallas_call(kernel, name='relay', out_shape=jax.ShapeDtypeStruct((micr...  38.5 us
    reshape x1, local copies, waits for them, and re-layouts, body(): return result.reshape(1, micro, times, stations, width)  0.8 us

profile of v6, /device:TPU:111, one launch (start us, length us, event | category | flops | bytes accessed | tf_op | source)
XLA Modules:
  0.0 39.4 jit_solution(10348483499819198375)
XLA Ops:
  0.0 38.5 %relay.1 = bf16[2,32,2048]{2,1,0:T(8,128)(2,1)S(1)} custom-call(bf16[2,8,4,2048]{3,2,1,0:T(4,128)(2,1)} %sig_hbm.1, bf16[16,128,384]{2,1,0:T(8,128)(2,1)} %bitcast.1, s32[2,4]{1,0:T(2,128)} %start_hbm.1, s32[2,4]{1,0:T(2,128)} %pad_hbm.1), custom_call_target="tpu_custom_call" | custom-call | tf_op jit(solution)/shard_map/relay/pallas_call | solution.py:525
  38.6 0.8 %reshape.3 = bf16[1,2,8,4,2048]{4,3,2,1,0:T(4,128)(2,1)} reshape(bf16[2,32,2048]{2,1,0:T(8,128)(2,1)S(1)} %relay.1) | data formatting | bytes 524288 | tf_op jit(solution)/shard_map/reshape | solution.py:562

commit v7 on v6

--- a/solution.py
+++ b/solution.py
@@ -60,42 +60,42 @@
     sig_copy = pltpu.make_async_copy(sig_hbm, sig, in_sem.at[1])
     start_copy = pltpu.make_async_copy(start_hbm, start, in_sem.at[2])
     pad_copy = pltpu.make_async_copy(pad_hbm, pad, in_sem.at[3])
+    barrier = pltpu.get_barrier_semaphore()
+
+    def signal(device):
+        pl.semaphore_signal(barrier, inc=1, device_id=device, device_id_type=MESH)
+
+    def greet(section, place, rep):
+        is_late = (section == 0) & (place == 0) & (rep == 0)
+
+        @pl.when(jnp.logical_not(is_late & (s == 1)))
+        def _():
+            signal((section + number(is_late), place, rep))
+
+    left = jnp.maximum(j - 1, 0)
+    right = jnp.minimum(j + 1, count - 1)
+    has_left = j > 0
+    has_right = j < count - 1
+
+    @pl.when(active)
+    def _():
+        sides(lambda: greet(before, left, other), lambda: greet(before, right, other))
+        greet(before, j, other)
+        sides(lambda: greet(s, left, r), lambda: greet(s, right, r))
+
+        @pl.when(jnp.logical_not(first))
+        def _():
+            greet(before, j, r)
+            sides(lambda: greet(before, left, r), lambda: greet(before, right, r))
+
+    @pl.when(helper)
+    def _():
+        signal((s, left, r))
+
     sig_copy.start()
     w_copy.start()
     start_copy.start()
     pad_copy.start()
-
-    barrier = pltpu.get_barrier_semaphore()
-
-    def signal(device):
-        pl.semaphore_signal(barrier, inc=1, device_id=device, device_id_type=MESH)
-
-    def greet(section, place, rep):
-        is_late = (section == 0) & (place == 0) & (rep == 0)
-
-        @pl.when(jnp.logical_not(is_late & (s == 1)))
-        def _():
-            signal((section + number(is_late), place, rep))
-
-    left = jnp.maximum(j - 1, 0)
-    right = jnp.minimum(j + 1, count - 1)
-    has_left = j > 0
-    has_right = j < count - 1
-
-    @pl.when(active)
-    def _():
-        greet(before, j, other)
-        sides(lambda: greet(s, left, r), lambda: greet(s, right, r))
-        sides(lambda: greet(before, left, other), lambda: greet(before, right, other))
-
-        @pl.when(jnp.logical_not(first))
-        def _():
-            greet(before, j, r)
-            sides(lambda: greet(before, left, r), lambda: greet(before, right, r))
-
-    @pl.when(helper)
-    def _():
-        signal((s, left, r))
 
     def lanes(c):
         return pl.ds(c * GROUP * HEAD, GROUP * HEAD)

time: 39.5 us -> 39.7 us (level)
  no operation moved by 1% of the time
where the time goes in v7:
time: 39.7 us; the launch traced here: 39.5 us
  Pallas kernels  38.7 us (97%)
  local copies, waits for them, and re-layouts  0.8 us (2%)
    pallas_call x1, Pallas kernels, body(): pl.pallas_call(kernel, name='relay', out_shape=jax.ShapeDtypeStruct((micr...  38.7 us
    reshape x1, local copies, waits for them, and re-layouts, body(): return result.reshape(1, micro, times, stations, width)  0.8 us

profile of v7, /device:TPU:111, one launch (start us, length us, event | category | flops | bytes accessed | tf_op | source)
XLA Modules:
  0.0 39.5 jit_solution(9665621102423438245)
XLA Ops:
  0.0 38.7 %relay.1 = bf16[2,32,2048]{2,1,0:T(8,128)(2,1)S(1)} custom-call(bf16[2,8,4,2048]{3,2,1,0:T(4,128)(2,1)} %sig_hbm.1, bf16[16,128,384]{2,1,0:T(8,128)(2,1)} %bitcast.1, s32[2,4]{1,0:T(2,128)} %start_hbm.1, s32[2,4]{1,0:T(2,128)} %pad_hbm.1), custom_call_target="tpu_custom_call" | custom-call | tf_op jit(solution)/shard_map/relay/pallas_call | solution.py:525
  38.7 0.8 %reshape.3 = bf16[1,2,8,4,2048]{4,3,2,1,0:T(4,128)(2,1)} reshape(bf16[2,32,2048]{2,1,0:T(8,128)(2,1)S(1)} %relay.1) | data formatting | bytes 524288 | tf_op jit(solution)/shard_map/reshape | solution.py:562

commit v8 on v6

--- a/solution.py
+++ b/solution.py
@@ -415,6 +415,11 @@
             seed_copy(m).wait_recv()
 
         mine = folded(squares(t, m, near, every))
+
+        @pl.when((t == 0) & (m > 0))
+        def _():
+            out[m - 1] = res[0, m - 1]
+
         p_arrived(t, m, 2, 1)
         mine = mine + pin[t, 1, m, 2]
         project_near(t, m, inverse((mine, 0), (mine, 1), (mine, 2), (mine, 3)))
@@ -463,7 +468,7 @@
 
     @pl.when(active)
     def _():
-        out[...] = res[0]
+        out[micro - 1] = res[0, micro - 1]
 
         @pl.when(jnp.logical_not(helper))
         def _():

time: 39.5 us -> 39.5 us (level)
  no operation moved by 1% of the time
where the time goes in v8:
time: 39.5 us; the launch traced here: 39.4 us
  Pallas kernels  38.5 us (97%)
  local copies, waits for them, and re-layouts  0.8 us (2%)
    pallas_call x1, Pallas kernels, body(): pl.pallas_call(kernel, name='relay', out_shape=jax.ShapeDtypeStruct((micr...  38.5 us
    reshape x1, local copies, waits for them, and re-layouts, body(): return result.reshape(1, micro, times, stations, width)  0.8 us

profile of v8, /device:TPU:111, one launch (start us, length us, event | category | flops | bytes accessed | tf_op | source)
XLA Modules:
  0.0 39.4 jit_solution(13354341287294767383)
XLA Ops:
  0.0 38.5 %relay.1 = bf16[2,32,2048]{2,1,0:T(8,128)(2,1)S(1)} custom-call(bf16[2,8,4,2048]{3,2,1,0:T(4,128)(2,1)} %sig_hbm.1, bf16[16,128,384]{2,1,0:T(8,128)(2,1)} %bitcast.1, s32[2,4]{1,0:T(2,128)} %start_hbm.1, s32[2,4]{1,0:T(2,128)} %pad_hbm.1), custom_call_target="tpu_custom_call" | custom-call | tf_op jit(solution)/shard_map/relay/pallas_call | solution.py:530
  38.5 0.8 %reshape.3 = bf16[1,2,8,4,2048]{4,3,2,1,0:T(4,128)(2,1)} reshape(bf16[2,32,2048]{2,1,0:T(8,128)(2,1)S(1)} %relay.1) | data formatting | bytes 524288 | tf_op jit(solution)/shard_map/reshape | solution.py:567
